TPU v7x, 768 devices: a whole 4x8x12 slice. The times are simulated.
768 devices in a mesh: grp: 8 (over x, core), blk: 96 (over y, z).
Axes of the slice: x: 4, y: 8, z: 12, core: 2. Of those that a mesh axis runs over, the one named last changes fastest.
Arguments:
- fine_pops: float32 [8, 19, 1536, 256], P('grp', None, 'blk'), may hold values from 0.38 to 8.7, as said below
- fine_solid: float32 [8, 1536, 256], P('grp', 'blk'), may hold values from 0.05 to 0.6
- coarse_pops: float32 [8, 19, 768, 256], P('grp', None, 'blk'), may hold values from 0.38 to 8.7, as said below
- coarse_solid: float32 [8, 768, 256], P('grp', 'blk'), may hold values from 0.05 to 0.6
- coarse_slot: int32 [8], replicated, may hold values from 0 to 31, as said below
Outputs:
- fine_out: float32 [8, 19, 1536, 256], P('grp', None, 'blk')
- coarse_out: float32 [8, 19, 768, 256], P('grp', None, 'blk')
Inputs may be any that keep to these rules, and one draw needn't show every extreme that they name: `fine_pops`: each population is between 0.7 and 1.3 times 20 w_i. `coarse_pops`: each population is between 0.7 and 1.3 times 20 w_i. `coarse_slot`: the 8 entries are distinct, and 31 is one of them.
All inputs are finite; a program needn't handle non-finite values.
Results may differ from a plain program's by a relative error of at most 0.0001.
Values sent between devices are 32-bit elements; how exact they have to be, the bound alone decides.
A program may use at most 128 MiB of HBM per device.

v0:
```python
import jax
import jax.numpy as jnp
import numpy as np
from jax import lax
from jax.sharding import PartitionSpec as P

BX = 16


lattice_vel = np.array(
    [
        [0, 0, 0],
        [1, 0, 0],
        [-1, 0, 0],
        [0, 1, 0],
        [0, -1, 0],
        [0, 0, 1],
        [0, 0, -1],
        [1, 1, 0],
        [-1, -1, 0],
        [1, -1, 0],
        [-1, 1, 0],
        [1, 0, 1],
        [-1, 0, -1],
        [1, 0, -1],
        [-1, 0, 1],
        [0, 1, 1],
        [0, -1, -1],
        [0, 1, -1],
        [0, -1, 1],
    ]
)
lattice_weight = np.array([1.0 / 3.0] + [1.0 / 18.0] * 6 + [1.0 / 36.0] * 12)
opposite_index = [0, 2, 1, 4, 3, 6, 5, 8, 7, 10, 9, 12, 11, 14, 13, 16, 15, 18, 17]
tau_fine = 0.6
tau_coarse = 0.55


def with_halo(block, sides, width):
    for axis, dim in sides:
        count = lax.axis_size(axis)
        forward = [(i, i + 1) for i in range(count - 1)]
        forward.append((count - 1, 0))
        backward = [(target, source) for source, target in forward]
        low = lax.ppermute(
            lax.slice_in_dim(block, block.shape[dim] - width, None, axis=dim), axis, forward
        )
        high = lax.ppermute(lax.slice_in_dim(block, 0, width, axis=dim), axis, backward)
        block = jnp.concatenate([low, block, high], axis=dim)
    return block


def spread_table(table, populations):
    return jnp.asarray(table, populations.dtype).reshape((19,) + (1,) * (populations.ndim - 1))


def equilibrium(populations):
    density = jnp.sum(populations, axis=0)
    velocity = [
        jnp.sum(spread_table(lattice_vel[:, k], populations) * populations, axis=0) / density
        for k in range(3)
    ]
    projected = spread_table(lattice_vel[:, 0], populations) * velocity[0]
    projected = projected + spread_table(lattice_vel[:, 1], populations) * velocity[1]
    projected = projected + spread_table(lattice_vel[:, 2], populations) * velocity[2]
    speed_sq = velocity[0] * velocity[0] + velocity[1] * velocity[1] + velocity[2] * velocity[2]
    return (
        spread_table(lattice_weight, populations)
        * density
        * (1.0 + 3.0 * projected + 4.5 * projected * projected - 1.5 * speed_sq)
    )


def collide_cells(populations, solid, relax):
    equil = equilibrium(populations)
    mirrored = jnp.stack([populations[j] for j in opposite_index])
    return (
        populations
        - (1.0 - solid) * (populations - equil) / relax
        + solid * (mirrored - populations)
    )


def stream_cells(collided):
    xlength = collided.shape[1]
    zlength = collided.shape[2] // BX
    moved = []
    padded = with_halo(collided, (("blk", 1),), 1)
    for j in range(19):
        offset = 1 - int(lattice_vel[j, 0])
        moved.append(padded[j, offset : offset + xlength])
    rolled = []
    for j in range(19):
        planes = moved[j].reshape(xlength, BX, zlength)
        planes = jnp.roll(planes, (int(lattice_vel[j, 1]), int(lattice_vel[j, 2])), axis=(1, 2))
        rolled.append(planes.reshape(xlength, BX * zlength))
    return jnp.stack(rolled)


def per_device(fine_pops, fine_solid, coarse_pops, coarse_solid, coarse_slot):
    populations = fine_pops[0]
    solid = fine_solid[0]
    for substep in range(2):
        populations = stream_cells(collide_cells(populations, solid, tau_fine))
    xlength = populations.shape[1]
    zlength = populations.shape[2] // BX
    averaged = populations.reshape(19, xlength // 2, 2, BX // 2, 2, zlength // 2, 2).mean(
        axis=(2, 4, 6)
    )
    equil = equilibrium(averaged)
    restricted = (equil + 2.0 * tau_coarse / tau_fine * (averaged - equil)).reshape(
        19, xlength // 2, BX // 2 * (zlength // 2)
    )
    group = lax.axis_index("grp")
    groups = lax.axis_size("grp")
    slot_iota = jnp.arange(groups, dtype=jnp.int32)
    own_code = jnp.sum(jnp.where(slot_iota == group, coarse_slot, 0))
    wanted = group * 4 + jnp.arange(4, dtype=jnp.int32)
    selector = (slot_iota == own_code // 4).astype(jnp.float32)
    outgoing = selector[:, None, None, None] * restricted[None]
    incoming = lax.all_to_all(outgoing, "grp", split_axis=0, concat_axis=0, tiled=True)
    matches = (coarse_slot[None, :] == wanted[:, None]).astype(jnp.float32)
    arrived = jnp.sum(matches[:, :, None, None, None] * incoming[None], axis=1)
    present = jnp.any(coarse_slot[None, :] == wanted[:, None], axis=1)
    coarse = coarse_pops[0].reshape(19, xlength // 2, BX, zlength)
    half_y = BX // 2
    half_z = zlength // 2
    for quadrant in range(4):
        low_y = quadrant // 2 * half_y
        low_z = quadrant % 2 * half_z
        region = coarse[:, :, low_y : low_y + half_y, low_z : low_z + half_z]
        incoming_tile = arrived[quadrant].reshape(19, xlength // 2, half_y, half_z)
        coarse = coarse.at[:, :, low_y : low_y + half_y, low_z : low_z + half_z].set(
            jnp.where(present[quadrant], incoming_tile, region)
        )
    coarse = coarse.reshape(19, xlength // 2, BX * zlength)
    coarse = stream_cells(collide_cells(coarse, coarse_solid[0], tau_coarse))
    return (populations[None], coarse[None])


def solution(mesh):
    placed = (
        P("grp", None, "blk", None),
        P("grp", "blk", None),
        P("grp", None, "blk", None),
        P("grp", "blk", None),
        P(),
    )
    return jax.shard_map(
        per_device,
        mesh=mesh,
        in_specs=placed,
        out_specs=(P("grp", None, "blk", None), P("grp", None, "blk", None)),
        check_vma=False,
    )
```

profile of v0, /device:TPU:1, one launch (start us, length us, event | category | flops | bytes accessed | tf_op | source)
XLA Modules:
  0.0 398.2 jit_solution(16649076177837377851)
XLA Ops:
  18.6 18.0 %collective-permute-start.1 = (f32[19,1,256]{2,1,0:T(1,128)S(1)}, f32[19,1,256]{2,1,0:T(1,128)S(1)}, u32[]{:S(2)}, u32[]{:S(2)}) collective-permute-start(f32[19,1,256]{2,1,0:T(1,128)S(1)} %get-tuple-element.161), channel_id=1, source_target_pairs={{1,0},{2,1},{3,2},{4,3},{5,4},{6,5},{7,6},{8,7},{9,8},{10,9},{11,1... | collective-permute-start | bytes 58376 | tf_op jit(solution)/shard_map/ppermute | solution.py:48
  36.6 1.9 collective-permute-start
  61.1 1.9 collective-permute-start.2
  72.5 2.2 stack.78
  77.7 2.2 stack.68
  80.0 1.6 stack_reshape.172
  81.6 2.2 stack.67
  85.4 2.3 stack.66
  89.3 2.2 stack.65
  91.5 1.6 stack_reshape.169
  93.1 6.8 %collective-permute-start.3 = (f32[19,1,256]{2,1,0:T(1,128)}, f32[19,1,256]{2,1,0:T(1,128)S(1)}, u32[]{:S(2)}, u32[]{:S(2)}) collective-permute-start(f32[19,1,256]{2,1,0:T(1,128)} %get-tuple-element.144), channel_id=1, source_target_pairs={{1,0},{2,1},{3,2},{4,3},{5,4},{6,5},{7,6},{8,7},{9,8},{10,9},{11,1... | collective-permute-start | bytes 58376 | tf_op jit(solution)/shard_map/ppermute | solution.py:48
  139.7 2.0 stack.63
  141.7 2.0 stack.64
  143.8 2.5 constant_dynamic-update-slice_fusion.93
  146.2 2.4 constant_dynamic-update-slice_fusion.92
  148.6 2.3 constant_dynamic-update-slice_fusion.91
  150.9 2.3 constant_dynamic-update-slice_fusion.90
  153.2 2.3 constant_dynamic-update-slice_fusion.89
  155.5 2.3 constant_dynamic-update-slice_fusion.88
  157.8 2.3 constant_dynamic-update-slice_fusion.87
  160.2 2.4 constant_dynamic-update-slice_fusion.86
  162.6 2.3 constant_dynamic-update-slice_fusion.85
  164.8 2.3 constant_dynamic-update-slice_fusion.84
  176.0 8.0 %reduce_sum.357 = f32[19,8,8,8]{3,2,1,0:T(8,128)S(1)} reduce(f32[19,8,2,8,2,8,2]{6,5,4,3,2,1,0:T(8,128)} %constant_dynamic-update-slice_fusion.76, f32[]{:T(128)} %constant.160.clone.1), dimensions={2,4,6}, to_apply=%region_9.10 | reduce | flops 68096 | bytes 350212 | tf_op jit(solution)/shard_map/reduce_sum | solution.py:107
  188.6 5.8 %all-to-all-start = ((f32[8,1,9728]{2,1,0:T(1,128)}), f32[8,1,9728]{2,1,0:T(1,128)S(1)}, u32[]{:S(2)}, u32[]{:S(2)}) async-start(f32[8,1,9728]{2,1,0:T(1,128)} %reshape.628), calls=%async_computation | async-start | bytes 622592 | tf_op jit(solution)/shard_map/all_to_all | solution.py:121
  211.1 20.9 %scatter.14 = f32[19,8,16,16]{3,2,1,0:T(8,128)S(1)} dynamic-update-slice(f32[19,8,16,16]{3,2,1,0:T(8,128)S(1)} %reshape_squeeze.200, f32[19,8,8,8]{3,2,1,0:T(8,128)S(1)} %slice_select_fusion.3, s32[]{:T(128)} %constant.169.clone.1, s32[]{:T(128)} %constant.169.clone.1, s32[]{:T(128)} %constant.169.clone.1, s32[]{:T(128)} %constant.169.clone.1) | dynamic-update-slice | bytes 77828 | tf_op jit(solution)/shard_map/scatter | solution.py:133
  232.8 2.7 fusion
  235.6 62.0 %scatter.15 = f32[19,8,16,16]{3,2,1,0:T(8,128)S(1)} dynamic-update-slice(f32[19,8,16,16]{3,2,1,0:T(8,128)S(1)} %scatter.14, f32[19,8,8,8]{3,2,1,0:T(8,128)S(1)} %fusion, s32[]{:T(128)} %constant.169.clone.1, s32[]{:T(128)} %constant.169.clone.1, s32[]{:T(128)} %bitcast.36, s32[]{:T(128)} %bitcast.37) | dynamic-update-slice | bytes 77828 | tf_op jit(solution)/shard_map/scatter | solution.py:133
  300.1 18.8 %scatter.16 = f32[19,8,16,16]{3,2,1,0:T(8,128)S(1)} dynamic-update-slice(f32[19,8,16,16]{3,2,1,0:T(8,128)S(1)} %scatter.15, f32[19,8,8,8]{3,2,1,0:T(8,128)S(1)} %slice_select_fusion.1, s32[]{:T(128)} %constant.169.clone.1, s32[]{:T(128)} %constant.169.clone.1, s32[]{:T(128)} %constant.177.clone.1, s32[]{:T(128)} %constant.169.clone.1) | dynamic-update-slice | bytes 77828 | tf_op jit(solution)/shard_map/scatter | solution.py:133
  319.8 59.0 %scatter.19 = f32[19,8,16,16]{3,2,1,0:T(8,128)S(1)} dynamic-update-slice(f32[19,8,16,16]{3,2,1,0:T(8,128)S(1)} %scatter.16, f32[19,8,8,8]{3,2,1,0:T(8,128)S(1)} %slice_select_fusion, s32[]{:T(128)} %constant.169.clone.1, s32[]{:T(128)} %constant.169.clone.1, s32[]{:T(128)} %constant.177.clone.1, s32[]{:T(128)} %constant.177.clone.1) | dynamic-update-slice | bytes 77828 | tf_op jit(solution)/shard_map/scatter | solution.py:133
  382.6 1.9 collective-permute-start.4
  384.6 7.2 %collective-permute-start.5 = (f32[19,1,256]{2,1,0:T(1,128)S(1)}, f32[19,1,256]{2,1,0:T(1,128)S(1)}, u32[]{:S(2)}, u32[]{:S(2)}) collective-permute-start(f32[19,1,256]{2,1,0:T(1,128)S(1)} %get-tuple-element.185), channel_id=1, source_target_pairs={{1,0},{2,1},{3,2},{4,3},{5,4},{6,5},{7,6},{8,7},{9,8},{10,9},{11,1... | collective-permute-start | bytes 58376 | tf_op jit(solution)/shard_map/ppermute | solution.py:48
  (497 shorter events, 135.5 us)
Async XLA Ops:
  0.6 55.5 %copy-start.26 = (f32[19]{0:T(128)S(1)}, f32[19]{0:T(128)}, u32[]{:S(2)}) copy-start(f32[19]{0:T(128)} %constant.181.clone) | copy-start | bytes 232
  0.6 55.5 %copy-start.28 = (f32[19]{0:T(128)S(1)}, f32[19]{0:T(128)}, u32[]{:S(2)}) copy-start(f32[19]{0:T(128)} %constant.182.clone) | copy-start | bytes 232
  0.7 55.5 %copy-start.30 = (f32[19]{0:T(128)S(1)}, f32[19]{0:T(128)}, u32[]{:S(2)}) copy-start(f32[19]{0:T(128)} %constant.183.clone) | copy-start | bytes 232
  0.7 55.7 %copy-start.32 = (f32[19]{0:T(128)S(1)}, f32[19]{0:T(128)}, u32[]{:S(2)}) copy-start(f32[19]{0:T(128)} %constant.184.clone) | copy-start | bytes 232
  0.7 55.7 %copy-start.13 = (f32[1,16,256]{2,1,0:T(8,128)S(1)}, f32[1,16,256]{2,1,0:T(8,128)}, u32[]{:S(2)}) copy-start(f32[1,16,256]{2,1,0:T(8,128)} %param.42) | copy-start | bytes 49156
  18.6 31.1 %collective-permute-start.1 = (f32[19,1,256]{2,1,0:T(1,128)S(1)}, f32[19,1,256]{2,1,0:T(1,128)S(1)}, u32[]{:S(2)}, u32[]{:S(2)}) collective-permute-start(f32[19,1,256]{2,1,0:T(1,128)S(1)} %get-tuple-element.161), channel_id=1, source_target_pairs={{1,0},{2,1},{3,2},{4,3},{5,4},{6,5},{7,6},{8,7},{9,8},{10,9},{11,1... | collective-permute-start | bytes 58376 | tf_op jit(solution)/shard_map/ppermute | solution.py:48
  36.6 13.1 %collective-permute-start = (f32[19,1,256]{2,1,0:T(1,128)S(1)}, f32[19,1,256]{2,1,0:T(1,128)S(1)}, u32[]{:S(2)}, u32[]{:S(2)}) collective-permute-start(f32[19,1,256]{2,1,0:T(1,128)S(1)} %get-tuple-element.160), channel_id=1, source_target_pairs={{0,1},{1,2},{2,3},{3,4},{4,5},{5,6},{6,7},{7,8},{8,9},{9,10},{10,1... | collective-permute-start | bytes 58376 | tf_op jit(solution)/shard_map/ppermute | solution.py:45
  61.1 38.8 %collective-permute-start.2 = (f32[19,1,256]{2,1,0:T(1,128)}, f32[19,1,256]{2,1,0:T(1,128)}, u32[]{:S(2)}, u32[]{:S(2)}) collective-permute-start(f32[19,1,256]{2,1,0:T(1,128)} %get-tuple-element.145), channel_id=1, source_target_pairs={{0,1},{1,2},{2,3},{3,4},{4,5},{5,6},{6,7},{7,8},{8,9},{9,10},{10,1... | collective-permute-start | bytes 58376 | tf_op jit(solution)/shard_map/ppermute | solution.py:45
  93.1 8.3 %collective-permute-start.3 = (f32[19,1,256]{2,1,0:T(1,128)}, f32[19,1,256]{2,1,0:T(1,128)S(1)}, u32[]{:S(2)}, u32[]{:S(2)}) collective-permute-start(f32[19,1,256]{2,1,0:T(1,128)} %get-tuple-element.144), channel_id=1, source_target_pairs={{1,0},{2,1},{3,2},{4,3},{5,4},{6,5},{7,6},{8,7},{9,8},{10,9},{11,1... | collective-permute-start | bytes 58376 | tf_op jit(solution)/shard_map/ppermute | solution.py:48
  143.7 25.8 %copy-start.3 = (f32[1,8,2,8,2,8,2]{6,5,4,3,2,1,0:T(8,128)S(1)}, f32[1,8,2,8,2,8,2]{6,5,4,3,2,1,0:T(8,128)}, u32[]{:S(2)}) copy-start(f32[1,8,2,8,2,8,2]{6,5,4,3,2,1,0:T(8,128)} %stack.75) | copy-start | bytes 49156
  143.7 26.9 %copy-start.2 = (f32[1,8,2,8,2,8,2]{6,5,4,3,2,1,0:T(8,128)S(1)}, f32[1,8,2,8,2,8,2]{6,5,4,3,2,1,0:T(8,128)}, u32[]{:S(2)}) copy-start(f32[1,8,2,8,2,8,2]{6,5,4,3,2,1,0:T(8,128)} %stack.76) | copy-start | bytes 49156
  143.7 27.9 %copy-start.1 = (f32[1,8,2,8,2,8,2]{6,5,4,3,2,1,0:T(8,128)S(1)}, f32[1,8,2,8,2,8,2]{6,5,4,3,2,1,0:T(8,128)}, u32[]{:S(2)}) copy-start(f32[1,8,2,8,2,8,2]{6,5,4,3,2,1,0:T(8,128)} %stack.77) | copy-start | bytes 49156
  143.7 29.0 %copy-start = (f32[1,8,2,8,2,8,2]{6,5,4,3,2,1,0:T(8,128)S(1)}, f32[1,8,2,8,2,8,2]{6,5,4,3,2,1,0:T(8,128)}, u32[]{:S(2)}) copy-start(f32[1,8,2,8,2,8,2]{6,5,4,3,2,1,0:T(8,128)} %stack.78) | copy-start | bytes 49156
  168.3 26.2 %copy-start.18 = (f32[1,16,256]{2,1,0:T(8,128)S(1)}, f32[1,16,256]{2,1,0:T(8,128)}, u32[]{:S(2)}) copy-start(f32[1,16,256]{2,1,0:T(8,128)} %stack_reshape.169) | copy-start | bytes 49156
  168.3 26.8 %copy-start.17 = (f32[1,16,256]{2,1,0:T(8,128)S(1)}, f32[1,16,256]{2,1,0:T(8,128)}, u32[]{:S(2)}) copy-start(f32[1,16,256]{2,1,0:T(8,128)} %stack_reshape.170) | copy-start | bytes 49156
  168.3 27.4 %copy-start.16 = (f32[1,16,256]{2,1,0:T(8,128)S(1)}, f32[1,16,256]{2,1,0:T(8,128)}, u32[]{:S(2)}) copy-start(f32[1,16,256]{2,1,0:T(8,128)} %stack_reshape.171) | copy-start | bytes 49156
  168.3 28.0 %copy-start.15 = (f32[1,16,256]{2,1,0:T(8,128)S(1)}, f32[1,16,256]{2,1,0:T(8,128)}, u32[]{:S(2)}) copy-start(f32[1,16,256]{2,1,0:T(8,128)} %stack_reshape.172) | copy-start | bytes 49156
  168.3 32.6 %copy-start.23 = (f32[1,16,256]{2,1,0:T(8,128)S(1)}, f32[1,16,256]{2,1,0:T(8,128)}, u32[]{:S(2)}) copy-start(f32[1,16,256]{2,1,0:T(8,128)} %stack_reshape.176) | copy-start | bytes 49156
  168.3 33.2 %copy-start.22 = (f32[1,16,256]{2,1,0:T(8,128)S(1)}, f32[1,16,256]{2,1,0:T(8,128)}, u32[]{:S(2)}) copy-start(f32[1,16,256]{2,1,0:T(8,128)} %stack_reshape.177) | copy-start | bytes 49156
  168.3 33.8 %copy-start.21 = (f32[1,16,256]{2,1,0:T(8,128)S(1)}, f32[1,16,256]{2,1,0:T(8,128)}, u32[]{:S(2)}) copy-start(f32[1,16,256]{2,1,0:T(8,128)} %stack_reshape.178) | copy-start | bytes 49156
  168.3 34.4 %copy-start.20 = (f32[1,16,256]{2,1,0:T(8,128)S(1)}, f32[1,16,256]{2,1,0:T(8,128)}, u32[]{:S(2)}) copy-start(f32[1,16,256]{2,1,0:T(8,128)} %stack_reshape.179) | copy-start | bytes 49156
  168.3 35.0 %copy-start.19 = (f32[1,16,256]{2,1,0:T(8,128)S(1)}, f32[1,16,256]{2,1,0:T(8,128)}, u32[]{:S(2)}) copy-start(f32[1,16,256]{2,1,0:T(8,128)} %stack_reshape.180) | copy-start | bytes 49156
  168.3 35.6 %copy-start.14 = (f32[1,16,256]{2,1,0:T(8,128)S(1)}, f32[1,16,256]{2,1,0:T(8,128)}, u32[]{:S(2)}) copy-start(f32[1,16,256]{2,1,0:T(8,128)} %stack_reshape.181) | copy-start | bytes 49156
  176.0 202.9 %copy-start.27 = (f32[19]{0:T(128)S(1)}, f32[19]{0:T(128)}, u32[]{:S(2)}) copy-start(f32[19]{0:T(128)} %constant.181.clone) | copy-start | bytes 232
  176.0 202.9 %copy-start.29 = (f32[19]{0:T(128)S(1)}, f32[19]{0:T(128)}, u32[]{:S(2)}) copy-start(f32[19]{0:T(128)} %constant.182.clone) | copy-start | bytes 232
  176.0 202.9 %copy-start.31 = (f32[19]{0:T(128)S(1)}, f32[19]{0:T(128)}, u32[]{:S(2)}) copy-start(f32[19]{0:T(128)} %constant.183.clone) | copy-start | bytes 232
  184.0 198.4 %copy-start.24 = (f32[1,8,256]{2,1,0:T(8,128)S(1)}, f32[1,8,256]{2,1,0:T(8,128)}, u32[]{:S(2)}) copy-start(f32[1,8,256]{2,1,0:T(8,128)} %param.44) | copy-start | bytes 24580
  184.0 198.4 %copy-start.25 = (f32[8,256]{1,0:T(8,128)S(1)}, f32[8,256]{1,0:T(8,128)}, u32[]{:S(2)}) copy-start(f32[8,256]{1,0:T(8,128)} %subtract_bitcast_fusion.1) | copy-start | bytes 24580
  184.0 198.4 %copy-start.33 = (f32[19]{0:T(128)S(1)}, f32[19]{0:T(128)}, u32[]{:S(2)}) copy-start(f32[19]{0:T(128)} %constant.184.clone) | copy-start | bytes 232
  188.6 17.7 %all-to-all-start = ((f32[8,1,9728]{2,1,0:T(1,128)}), f32[8,1,9728]{2,1,0:T(1,128)S(1)}, u32[]{:S(2)}, u32[]{:S(2)}) async-start(f32[8,1,9728]{2,1,0:T(1,128)} %reshape.628), calls=%async_computation | async-start | bytes 622592 | tf_op jit(solution)/shard_map/all_to_all | solution.py:121
  382.6 9.2 %collective-permute-start.4 = (f32[19,1,256]{2,1,0:T(1,128)S(1)}, f32[19,1,256]{2,1,0:T(1,128)S(1)}, u32[]{:S(2)}, u32[]{:S(2)}) collective-permute-start(f32[19,1,256]{2,1,0:T(1,128)S(1)} %get-tuple-element.186), channel_id=1, source_target_pairs={{0,1},{1,2},{2,3},{3,4},{4,5},{5,6},{6,7},{7,8},{8,9},{9,10},{10,1... | collective-permute-start | bytes 58376 | tf_op jit(solution)/shard_map/ppermute | solution.py:45
  384.6 8.1 %collective-permute-start.5 = (f32[19,1,256]{2,1,0:T(1,128)S(1)}, f32[19,1,256]{2,1,0:T(1,128)S(1)}, u32[]{:S(2)}, u32[]{:S(2)}) collective-permute-start(f32[19,1,256]{2,1,0:T(1,128)S(1)} %get-tuple-element.185), channel_id=1, source_target_pairs={{1,0},{2,1},{3,2},{4,3},{5,4},{6,5},{7,6},{8,7},{9,8},{10,9},{11,1... | collective-permute-start | bytes 58376 | tf_op jit(solution)/shard_map/ppermute | solution.py:48
  (10 other events, 53.3 us)
where the time goes:
time: 402 us; the launch traced here: 398 us
  local copies, waits for them, and re-layouts  299 us (74%)
  other arithmetic  49.2 us (12%)
  starting transfers between devices  43.7 us (11%)
  between operations  5.8 us (1%)
    scatter x4, local copies, waits for them, and re-layouts, per_device(): coarse.at[:, :, low_y:low_y + half_y, low_z:low_z + half_z]  161 us
    unnamed x182, local copies, waits for them, and re-layouts  62 us
    another operation x71, local copies, waits for them, and re-layouts, stream_cells(): return jnp.stack(rolled)  49.1 us
    ppermute x3, starting transfers between devices, with_halo(): lax.ppermute(lax.slice_in_dim(block, 0, width, axis=dim), axis, backward)  32.1 us
    concatenate x60, other arithmetic, stream_cells(): jnp.roll(planes, (int(lattice_vel[j, 1]), int(lattice_vel[j, 2])), axis=(...  16.9 us
    another operation x48, local copies, waits for them, and re-layouts, stream_cells(): planes = moved[j].reshape(xlength, BX, zlength)  9.85 us
  transfers between devices with their start and end apart: 7, of which 1 were waited for; matrix products, arithmetic and copies ran while one was open for 13% of the time, Pallas kernels for 0%

commit v1 on v0

v1 whole, which is shorter than its diff:
```python
import jax
import jax.numpy as jnp
import numpy as np
from jax import lax
from jax.experimental import pallas as pl
from jax.experimental.pallas import tpu as pltpu
from jax.sharding import PartitionSpec as P

MESH = pl.DeviceIdType.MESH
F32 = jnp.float32

lattice_vel = [
    (0, 0, 0), (1, 0, 0), (-1, 0, 0), (0, 1, 0), (0, -1, 0), (0, 0, 1), (0, 0, -1),
    (1, 1, 0), (-1, -1, 0), (1, -1, 0), (-1, 1, 0), (1, 0, 1), (-1, 0, -1),
    (1, 0, -1), (-1, 0, 1), (0, 1, 1), (0, -1, -1), (0, 1, -1), (0, -1, 1),
]
tau_fine = 0.6
tau_coarse = 0.55
rescale = 2.0 * tau_coarse / tau_fine
RIGHT = [i for i in range(19) if lattice_vel[i][0] == 1]
LEFT = [i for i in range(19) if lattice_vel[i][0] == -1]
STAY = [i for i in range(19) if lattice_vel[i][0] == 0]
X = 16
C = 8
PAD = 8
HALVES = (0, 128)


def relaxed(f, keep_even, keep_odd, a):
    even = [None] * 19
    odd = [None] * 19
    for i in range(1, 19, 2):
        even[i] = f[i] + f[i + 1]
        odd[i] = f[i] - f[i + 1]
    rho = f[0]
    for i in range(1, 19, 2):
        rho = rho + even[i]
    j = []
    for axis in range(3):
        total = None
        for i in range(1, 19, 2):
            c = lattice_vel[i][axis]
            if c:
                term = odd[i]
                if total is None:
                    total = term if c > 0 else -term
                else:
                    total = total + term if c > 0 else total - term
        j.append(total)
    inverse = 1.0 / rho
    q = a * inverse
    jj = j[0] * j[0] + j[1] * j[1] + j[2] * j[2]
    base = a * rho - (1.5 * q) * jj
    out = [None] * 19
    out[0] = 2.0 * keep_even * f[0] + (1.0 / 3.0) * base
    axis_base = (1.0 / 18.0) * base
    edge_base = (1.0 / 36.0) * base
    axis_q = (4.5 / 18.0) * q
    edge_q = (4.5 / 36.0) * q
    axis_a = (3.0 / 18.0) * a
    edge_a = (3.0 / 36.0) * a
    for i in range(1, 19, 2):
        cj = None
        for axis in range(3):
            c = lattice_vel[i][axis]
            if c:
                if cj is None:
                    cj = j[axis] if c > 0 else -j[axis]
                else:
                    cj = cj + j[axis] if c > 0 else cj - j[axis]
        if i < 7:
            e = axis_base + axis_q * (cj * cj) + keep_even * even[i]
            o = axis_a * cj + keep_odd * odd[i]
        else:
            e = edge_base + edge_q * (cj * cj) + keep_even * even[i]
            o = edge_a * cj + keep_odd * odd[i]
        out[i] = e + o
        out[i + 1] = e - o
    return out


def collide(f, solid, tau):
    a = (1.0 - solid) * (1.0 / tau)
    keep_even = 0.5 * (1.0 - a)
    return relaxed(f, keep_even, keep_even - solid, a)


def lane_shift(low, high, cy, cz, lane):
    if cy == 0 and cz == 0:
        return low, high
    shift = 16 * cy + cz
    parts = []
    for v in (low, high):
        moved = pltpu.roll(v, shift % 128, 1)
        if cz:
            wrapped = pltpu.roll(v, (shift - 16 * cz) % 128, 1)
            z = lane % 16
            moved = jnp.where(z == (0 if cz > 0 else 15), wrapped, moved)
        parts.append(moved)
    if cy == 0:
        return parts[0], parts[1]
    crossing = lane < 16 if cy > 0 else lane >= 112
    return jnp.where(crossing, parts[1], parts[0]), jnp.where(crossing, parts[0], parts[1])


def lanes(rows):
    return lax.broadcasted_iota(jnp.int32, (rows, 128), 1)


def streamed(source, row, rows):
    lane = lanes(rows)
    low, high = [], []
    for i in range(19):
        cx, cy, cz = lattice_vel[i]
        start = row - cx
        a = source[i, start : start + rows, 0:128]
        b = source[i, start : start + rows, 128:256]
        a, b = lane_shift(a, b, cy, cz, lane)
        low.append(a)
        high.append(b)
    return low, high


def kernel(
    groups, blocks, slot_ref, fine_hbm, solid_hbm, coarse_hbm, csolid_hbm, fine_out, coarse_out,
    fine, solid, coarse, csolid, first, second, moved, averaged, boxes, paste, settled, cmoved,
    to_right, to_left, from_left, from_right, cto_right, cto_left, cfrom_left, cfrom_right,
    load_sem, store_sem, halo_send, halo_recv, box_send, box_recv, chalo_send, chalo_recv,
):
    g = lax.axis_index("grp")
    b = lax.axis_index("blk")
    right = (g, lax.rem(b + 1, blocks))
    left = (g, lax.rem(b + blocks - 1, blocks))
    peers = [(lax.rem(g + d, groups), b) for d in range(1, groups)]

    loads = [
        pltpu.make_async_copy(fine_hbm.at[0], fine, load_sem.at[0]),
        pltpu.make_async_copy(solid_hbm.at[0], solid.at[PAD : PAD + X], load_sem.at[1]),
        pltpu.make_async_copy(coarse_hbm.at[0], coarse, load_sem.at[2]),
        pltpu.make_async_copy(csolid_hbm.at[0], csolid, load_sem.at[3]),
    ]
    for load in loads:
        load.start()
    barrier = pltpu.get_barrier_semaphore()
    for device in [left, right] + peers:
        pl.semaphore_signal(barrier, inc=1, device_id=device, device_id_type=MESH)

    row = lax.broadcasted_iota(jnp.int32, (256, 128), 0)
    column = lax.broadcasted_iota(jnp.int32, (256, 128), 1)
    hit = (row // 32 == column // 16) & ((row % 16) // 2 == column % 8)
    boxes[...] = jnp.where(hit, 0.125, 0.0).astype(jnp.bfloat16)

    loads[0].wait()
    loads[1].wait()
    for t in range(X // 8):
        for h in HALVES:
            span = slice(h, h + 128)
            f = [fine[i, 8 * t : 8 * t + 8, span] for i in range(19)]
            s = solid[PAD + 8 * t : PAD + 8 * t + 8, span]
            f = collide(f, s, tau_fine)
            for i in range(19):
                first[i, PAD + 8 * t : PAD + 8 * t + 8, span] = f[i]
            if t == 0:
                for k, i in enumerate(LEFT):
                    to_left[k : k + 1, span] = f[i][1:2]
                for k, i in enumerate(LEFT + STAY):
                    to_left[5 + k : 6 + k, span] = f[i][0:1]
                to_left[19:20, span] = s[0:1]
            if t == X // 8 - 1:
                for k, i in enumerate(RIGHT):
                    to_right[k : k + 1, span] = f[i][6:7]
                for k, i in enumerate(RIGHT + STAY):
                    to_right[5 + k : 6 + k, span] = f[i][7:8]
                to_right[19:20, span] = s[7:8]

    pl.semaphore_wait(barrier, groups + 1)
    halos = [
        pltpu.make_async_remote_copy(
            to_right, from_left, halo_send.at[0], halo_recv.at[0], right, MESH),
        pltpu.make_async_remote_copy(
            to_left, from_right, halo_send.at[1], halo_recv.at[1], left, MESH),
    ]
    for halo in halos:
        halo.start()

    def second_collision(start, rows):
        low, high = streamed(first, start, rows)
        for f, h in ((low, 0), (high, 128)):
            span = slice(h, h + 128)
            f = collide(f, solid[start : start + rows, span], tau_fine)
            for i in range(19):
                second[i, start : start + rows, span] = f[i]

    def second_stream(start, rows):
        low, high = streamed(second, start, rows)
        for i in range(19):
            moved[0, i, start - PAD : start - PAD + rows, :] = low[i]
            moved[1, i, start - PAD : start - PAD + rows, :] = high[i]

    for t in range(X // 8):
        second_collision(PAD + 8 * t, 8)
    for t in range(X // 8):
        second_stream(PAD + 8 * t, 8)

    for halo in halos:
        halo.wait_recv()
    for k, i in enumerate(RIGHT):
        first[i, PAD - 2 : PAD - 1, :] = from_left[k : k + 1, :]
    for k, i in enumerate(RIGHT + STAY):
        first[i, PAD - 1 : PAD, :] = from_left[5 + k : 6 + k, :]
    solid[PAD - 1 : PAD, :] = from_left[19:20, :]
    for k, i in enumerate(LEFT):
        first[i, PAD + X + 1 : PAD + X + 2, :] = from_right[k : k + 1, :]
    for k, i in enumerate(LEFT + STAY):
        first[i, PAD + X : PAD + X + 1, :] = from_right[5 + k : 6 + k, :]
    solid[PAD + X : PAD + X + 1, :] = from_right[19:20, :]
    second_collision(PAD - 1, 2)
    second_collision(PAD + X - 1, 2)
    second_stream(PAD, 2)
    second_stream(PAD + X - 2, 2)
    stores = [
        pltpu.make_async_copy(moved.at[k], fine_out.at[0, :, :, h : h + 128], store_sem.at[k])
        for k, h in enumerate(HALVES)
    ]
    for store in stores:
        store.start()

    for i in range(19):
        for k, h in enumerate(HALVES):
            averaged[8 * i : 8 * i + 8, h : h + 128] = (
                moved[k, i, pl.ds(0, 8, stride=2), :] + moved[k, i, pl.ds(1, 8, stride=2), :])
    rest = averaged[...]
    total = None
    for part in range(3):
        piece = rest.astype(jnp.bfloat16)
        product = jnp.dot(piece, boxes[...], preferred_element_type=F32)
        total = product if total is None else total + product
        if part < 2:
            rest = rest - piece.astype(F32)
    a = jnp.full((8, 128), 1.0 - rescale, F32)
    keep = jnp.full((8, 128), 0.5 * rescale, F32)
    f = relaxed([total[8 * i : 8 * i + 8] for i in range(19)], keep, keep, a)
    lane = lanes(8)
    near = lane % 16 < 8
    for k in range(10):
        paste[g, k] = jnp.where(near, f[2 * k], f[min(2 * k + 1, 18)])
    sends = []
    for d, peer in enumerate(peers):
        sends.append(pltpu.make_async_remote_copy(
            paste.at[g], paste.at[g], box_send.at[d], box_recv.at[g], peer, MESH))
    for send in sends:
        send.start()

    loads[2].wait()
    loads[3].wait()
    sources, present = [], []
    for q in range(4):
        source = jnp.int32(0)
        found = jnp.int32(0)
        for k in range(groups):
            match = (slot_ref[k] == 4 * g + q).astype(jnp.int32)
            source = jnp.maximum(source, k * match)
            found = jnp.maximum(found, match)
        sources.append(source)
        present.append(found)
    for d, peer in enumerate(peers):
        pltpu.make_async_remote_copy(
            paste.at[peer[0]], paste.at[peer[0]], box_send.at[d], box_recv.at[peer[0]], peer, MESH
        ).wait_recv()
    for half, h in enumerate(HALVES):
        span = slice(h, h + 128)
        one, two = sources[2 * half], sources[2 * half + 1]
        put = jnp.where(
            near,
            jnp.full((8, 128), present[2 * half], jnp.int32),
            jnp.full((8, 128), present[2 * half + 1], jnp.int32),
        ) > 0
        f = []
        for k in range(10):
            tile_one, tile_two = paste[one, k], paste[two, k]
            i = 2 * k
            value = jnp.where(near, tile_one, pltpu.roll(tile_two, 8, 1))
            f.append(jnp.where(put, value, coarse[i, :, span]))
            if i + 1 < 19:
                value = jnp.where(near, pltpu.roll(tile_one, 120, 1), tile_two)
                f.append(jnp.where(put, value, coarse[i + 1, :, span]))
        f = collide(f, csolid[:, span], tau_coarse)
        for i in range(19):
            settled[i, PAD : PAD + C, span] = f[i]
        for k, i in enumerate(LEFT):
            cto_left[k : k + 1, span] = f[i][0:1]
        for k, i in enumerate(RIGHT):
            cto_right[k : k + 1, span] = f[i][7:8]
    chalos = [
        pltpu.make_async_remote_copy(
            cto_right, cfrom_left, chalo_send.at[0], chalo_recv.at[0], right, MESH),
        pltpu.make_async_remote_copy(
            cto_left, cfrom_right, chalo_send.at[1], chalo_recv.at[1], left, MESH),
    ]
    for halo in chalos:
        halo.start()
    for halo in chalos:
        halo.wait_recv()
    for k, i in enumerate(RIGHT):
        settled[i, PAD - 1 : PAD, :] = cfrom_left[k : k + 1, :]
    for k, i in enumerate(LEFT):
        settled[i, PAD + C : PAD + C + 1, :] = cfrom_right[k : k + 1, :]
    low, high = streamed(settled, PAD, C)
    for i in range(19):
        cmoved[i, :, 0:128] = low[i]
        cmoved[i, :, 128:256] = high[i]
    stores.append(pltpu.make_async_copy(cmoved, coarse_out.at[0], store_sem.at[2]))
    stores[2].start()
    for copy in halos + sends + chalos:
        copy.wait_send()
    for store in stores:
        store.wait()


def solution(mesh):
    groups, blocks = mesh.shape["grp"], mesh.shape["blk"]

    def per_device(fine_pops, fine_solid, coarse_pops, coarse_solid, coarse_slot):
        body = lambda *refs: kernel(groups, blocks, *refs)
        return pl.pallas_call(
            body,
            out_shape=(
                jax.ShapeDtypeStruct(fine_pops.shape, F32),
                jax.ShapeDtypeStruct(coarse_pops.shape, F32),
            ),
            in_specs=[pl.BlockSpec(memory_space=pltpu.SMEM)]
            + [pl.BlockSpec(memory_space=pl.ANY)] * 4,
            out_specs=(pl.BlockSpec(memory_space=pl.ANY), pl.BlockSpec(memory_space=pl.ANY)),
            scratch_shapes=[
                pltpu.VMEM((19, X, 256), F32),
                pltpu.VMEM((X + 2 * PAD, 256), F32),
                pltpu.VMEM((19, C, 256), F32),
                pltpu.VMEM((C, 256), F32),
                pltpu.VMEM((19, X + 2 * PAD, 256), F32),
                pltpu.VMEM((19, X + 2 * PAD, 256), F32),
                pltpu.VMEM((2, 19, X, 128), F32),
                pltpu.VMEM((19 * 8, 256), F32),
                pltpu.VMEM((256, 128), jnp.bfloat16),
                pltpu.VMEM((groups, 10, 8, 128), F32),
                pltpu.VMEM((19, C + 2 * PAD, 256), F32),
                pltpu.VMEM((19, C, 256), F32),
                pltpu.VMEM((24, 256), F32),
                pltpu.VMEM((24, 256), F32),
                pltpu.VMEM((24, 256), F32),
                pltpu.VMEM((24, 256), F32),
                pltpu.VMEM((8, 256), F32),
                pltpu.VMEM((8, 256), F32),
                pltpu.VMEM((8, 256), F32),
                pltpu.VMEM((8, 256), F32),
                pltpu.SemaphoreType.DMA((4,)),
                pltpu.SemaphoreType.DMA((3,)),
                pltpu.SemaphoreType.DMA((2,)),
                pltpu.SemaphoreType.DMA((2,)),
                pltpu.SemaphoreType.DMA((groups,)),
                pltpu.SemaphoreType.DMA((groups,)),
                pltpu.SemaphoreType.DMA((2,)),
                pltpu.SemaphoreType.DMA((2,)),
            ],
            compiler_params=pltpu.CompilerParams(collective_id=0, has_side_effects=True),
        )(coarse_slot, fine_pops, fine_solid, coarse_pops, coarse_solid)

    placed = (
        P("grp", None, "blk", None),
        P("grp", "blk", None),
        P("grp", None, "blk", None),
        P("grp", "blk", None),
        P(),
    )
    return jax.shard_map(
        per_device,
        mesh=mesh,
        in_specs=placed,
        out_specs=(P("grp", None, "blk", None), P("grp", None, "blk", None)),
        check_vma=False,
    )
```

time: 402 us -> 37.2 us (0.09)
  local copies, waits for them, and re-layouts: 299 us -> 2.41 us
  other arithmetic: 49.2 us -> 0 us
  starting transfers between devices: 43.7 us -> 0 us
  Pallas kernels: 0 us -> 33.9 us
  between operations: 5.8 us -> 0.65 us
    scatter x4 -> x0, local copies, waits for them, and re-layouts: 161 us -> none  [per_device(): coarse.at[:, :, low_y:low_y + half_y, low_z:low_z + half_z]]
    another operation x128 -> x0, local copies, waits for them, and re-layouts: 64.4 us -> none  [the longest x71 49.1 us: stream_cells(): return jnp.stack(rolled)]
    unnamed x182 -> x4, local copies, waits for them, and re-layouts: 62 us -> 2.41 us
    ppermute x6 -> x0, starting transfers between devices: 37.9 us -> none  [the longest x3 32.1 us: with_halo(): lax.ppermute(lax.slice_in_dim(block, 0, width, axis=dim), axis, backward)]
    pallas_call x0 -> x1, Pallas kernels: none -> 33.9 us  [per_device(): pl.pallas_call(body, out_shape=(jax.ShapeDtypeStruct(fine_pops.shape, F32...]
    concatenate x64 -> x0, other arithmetic: 19.8 us -> none  [the longest x60 16.9 us: stream_cells(): jnp.roll(planes, (int(lattice_vel[j, 1]), int(lattice_vel[j, 2])), axis=(...]
    reduce_sum x8 -> x0, other arithmetic: 14.1 us -> none  [the longest x1 8.01 us: per_device(): populations.reshape(19, xlength // 2, 2, BX // 2, 2, zlength // 2, 2)]
    slice x93 -> x0, local copies, waits for them, and re-layouts: 9.56 us -> none  [the longest x63 5.08 us: stream_cells(): jnp.roll(planes, (int(lattice_vel[j, 1]), int(lattice_vel[j, 2])), axis=(...]
  transfers between devices with their start and end apart: 7 -> 0, of which waited for: 1 -> 0; matrix products, arithmetic and copies ran while one was open for 13% -> 0% of each run, Pallas kernels for 0% -> 0%
where the time goes in v1:
time: 37.2 us; the launch traced here: 37 us
  Pallas kernels  33.9 us (91%)
  local copies, waits for them, and re-layouts  2.41 us (6%)
  between operations  0.65 us (2%)
    pallas_call x1, Pallas kernels, per_device(): pl.pallas_call(body, out_shape=(jax.ShapeDtypeStruct(fine_pops.shape, F32...  33.9 us
    unnamed x4, local copies, waits for them, and re-layouts  2.41 us

profile of v1, /device:TPU:1, one launch (start us, length us, event | category | flops | bytes accessed | tf_op | source)
XLA Modules:
  0.0 37.0 jit_solution(10236188488227183169)
XLA Ops:
  0.6 33.9 %shard_map.68 = (f32[1,19,16,256]{3,2,1,0:T(8,128)}, f32[1,19,8,256]{3,2,1,0:T(8,128)}) custom-call(s32[8]{0:T(128)} %refs_0_.1, f32[1,19,16,256]{3,2,1,0:T(8,128)} %refs_1_.1, f32[1,16,256]{2,1,0:T(8,128)} %refs_2_.1, f32[1,19,8,256]{3,2,1,0:T(8,128)} %refs_3_.1, f32[1,8,256]{2,1,0:T(8,128)} %refs_4_.1), custom_call_target="tpu_custom_call" | custom-call | tf_op jit(solution)/shard_map/pallas_call | solution.py:325
  34.6 0.0 copy-start
  34.6 1.7 %copy.9 = f32[1,19,16,256]{3,2,1,0:T(8,128)} copy(f32[1,19,16,256]{3,2,1,0:T(8,128)} %get-tuple-element.4) | data formatting | bytes 622592
  36.3 0.0 copy-done
  36.3 0.7 %copy.10 = f32[1,19,8,256]{3,2,1,0:T(8,128)} copy(f32[1,19,8,256]{3,2,1,0:T(8,128)S(1)} %copy-done) | data formatting | bytes 311296
Async XLA Ops:
  34.6 1.8 %copy-start = (f32[1,19,8,256]{3,2,1,0:T(8,128)S(1)}, f32[1,19,8,256]{3,2,1,0:T(8,128)}, u32[]{:S(2)}) copy-start(f32[1,19,8,256]{3,2,1,0:T(8,128)} %get-tuple-element.5) | copy-start | bytes 466948

commit v2 on v1

v2 whole, which is shorter than its diff:
```python
import jax
import jax.numpy as jnp
import numpy as np
from jax import lax
from jax.experimental import pallas as pl
from jax.experimental.pallas import tpu as pltpu
from jax.sharding import PartitionSpec as P

MESH = pl.DeviceIdType.MESH
F32 = jnp.float32

lattice_vel = [
    (0, 0, 0), (1, 0, 0), (-1, 0, 0), (0, 1, 0), (0, -1, 0), (0, 0, 1), (0, 0, -1),
    (1, 1, 0), (-1, -1, 0), (1, -1, 0), (-1, 1, 0), (1, 0, 1), (-1, 0, -1),
    (1, 0, -1), (-1, 0, 1), (0, 1, 1), (0, -1, -1), (0, 1, -1), (0, -1, 1),
]
tau_fine = 0.6
tau_coarse = 0.55
rescale = 2.0 * tau_coarse / tau_fine
RIGHT = [i for i in range(19) if lattice_vel[i][0] == 1]
LEFT = [i for i in range(19) if lattice_vel[i][0] == -1]
STAY = [i for i in range(19) if lattice_vel[i][0] == 0]
X = 16
C = 8
PAD = 8
HALVES = (0, 128)


def relaxed(f, keep_even, keep_odd, a):
    even = [None] * 19
    odd = [None] * 19
    for i in range(1, 19, 2):
        even[i] = f[i] + f[i + 1]
        odd[i] = f[i] - f[i + 1]
    rho = f[0]
    for i in range(1, 19, 2):
        rho = rho + even[i]
    j = []
    for axis in range(3):
        total = None
        for i in range(1, 19, 2):
            c = lattice_vel[i][axis]
            if c:
                term = odd[i]
                if total is None:
                    total = term if c > 0 else -term
                else:
                    total = total + term if c > 0 else total - term
        j.append(total)
    inverse = 1.0 / rho
    q = a * inverse
    jj = j[0] * j[0] + j[1] * j[1] + j[2] * j[2]
    base = a * rho - (1.5 * q) * jj
    out = [None] * 19
    out[0] = 2.0 * keep_even * f[0] + (1.0 / 3.0) * base
    axis_base = (1.0 / 18.0) * base
    edge_base = (1.0 / 36.0) * base
    axis_q = (4.5 / 18.0) * q
    edge_q = (4.5 / 36.0) * q
    axis_a = (3.0 / 18.0) * a
    edge_a = (3.0 / 36.0) * a
    for i in range(1, 19, 2):
        cj = None
        for axis in range(3):
            c = lattice_vel[i][axis]
            if c:
                if cj is None:
                    cj = j[axis] if c > 0 else -j[axis]
                else:
                    cj = cj + j[axis] if c > 0 else cj - j[axis]
        if i < 7:
            e = axis_base + axis_q * (cj * cj) + keep_even * even[i]
            o = axis_a * cj + keep_odd * odd[i]
        else:
            e = edge_base + edge_q * (cj * cj) + keep_even * even[i]
            o = edge_a * cj + keep_odd * odd[i]
        out[i] = e + o
        out[i + 1] = e - o
    return out


def collide(f, solid, tau):
    a = (1.0 - solid) * (1.0 / tau)
    keep_even = 0.5 * (1.0 - a)
    return relaxed(f, keep_even, keep_even - solid, a)


def lane_shift(low, high, cy, cz, lane):
    if cy == 0 and cz == 0:
        return low, high
    shift = 16 * cy + cz
    parts = []
    for v in (low, high):
        moved = pltpu.roll(v, shift % 128, 1)
        if cz:
            wrapped = pltpu.roll(v, (shift - 16 * cz) % 128, 1)
            z = lane % 16
            moved = jnp.where(z == (0 if cz > 0 else 15), wrapped, moved)
        parts.append(moved)
    if cy == 0:
        return parts[0], parts[1]
    crossing = lane < 16 if cy > 0 else lane >= 112
    return jnp.where(crossing, parts[1], parts[0]), jnp.where(crossing, parts[0], parts[1])


def lanes(rows):
    return lax.broadcasted_iota(jnp.int32, (rows, 128), 1)


def streamed(source, row, rows):
    lane = lanes(rows)
    low, high = [], []
    for i in range(19):
        cx, cy, cz = lattice_vel[i]
        start = row - cx
        a = source[i, start : start + rows, 0:128]
        b = source[i, start : start + rows, 128:256]
        a, b = lane_shift(a, b, cy, cz, lane)
        low.append(a)
        high.append(b)
    return low, high


def kernel(
    groups, blocks, slot_ref, fine_hbm, solid_hbm, coarse_hbm, csolid_hbm, moved, settled,
    fine, solid, coarse, csolid, first, second, edge, boxes, inner, outer_r, outer_l,
    to_right, to_left, from_left, from_right, cto_right, cto_left, cfrom_left, cfrom_right,
    load_sem, ready, halo_send, halo_recv, chalo_send, chalo_recv, box_send, box_recv,
):
    g = lax.axis_index("grp")
    b = lax.axis_index("blk")
    right = (g, lax.rem(b + 1, blocks))
    left = (g, lax.rem(b + blocks - 1, blocks))
    peers = [(lax.rem(g + d, groups), b) for d in (4, 3, 5, 2, 6, 1, 7)]

    loads = [
        pltpu.make_async_copy(solid_hbm.at[0], solid.at[PAD : PAD + X], load_sem.at[0]),
        pltpu.make_async_copy(fine_hbm.at[0, :, 8:16], fine.at[:, 8:16], load_sem.at[1]),
        pltpu.make_async_copy(fine_hbm.at[0, :, 0:8], fine.at[:, 0:8], load_sem.at[2]),
        pltpu.make_async_copy(csolid_hbm.at[0], csolid.at[PAD : PAD + C], load_sem.at[3]),
        pltpu.make_async_copy(coarse_hbm.at[0], coarse.at[:, PAD : PAD + C], load_sem.at[4]),
    ]
    for load in loads:
        load.start()
    barrier = pltpu.get_barrier_semaphore()
    for device in [left] + peers:
        pl.semaphore_signal(barrier, inc=1, device_id=device, device_id_type=MESH)

    def first_collision(t):
        out = []
        for h in HALVES:
            span = slice(h, h + 128)
            f = [fine[i, 8 * t : 8 * t + 8, span] for i in range(19)]
            f = collide(f, solid[PAD + 8 * t : PAD + 8 * t + 8, span], tau_fine)
            for i in range(19):
                first[i, PAD + 8 * t : PAD + 8 * t + 8, span] = f[i]
            out.append(f)
        return out

    loads[0].wait()
    loads[1].wait()
    for f, h in zip(first_collision(1), HALVES):
        span = slice(h, h + 128)
        for k, i in enumerate(RIGHT + STAY):
            to_right[4 * k : 4 * k + 4, span] = f[i][4:8]
        to_right[56:60, span] = solid[PAD + 12 : PAD + 16, span]
        for k, i in enumerate(LEFT):
            to_right[60 + 2 * k : 62 + 2 * k, span] = f[i][6:8]
    pl.semaphore_wait(barrier, groups)
    halo_r = pltpu.make_async_remote_copy(
        to_right, from_left, halo_send.at[0], halo_recv.at[0], right, MESH)
    halo_r.start()
    pl.semaphore_signal(ready, inc=1, device_id=right, device_id_type=MESH)

    loads[2].wait()
    for f, h in zip(first_collision(0), HALVES):
        span = slice(h, h + 128)
        for k, i in enumerate(LEFT + STAY):
            to_left[4 * k : 4 * k + 4, span] = f[i][0:4]
        to_left[56:60, span] = solid[PAD : PAD + 4, span]
        for k, i in enumerate(RIGHT):
            to_left[60 + 2 * k : 62 + 2 * k, span] = f[i][0:2]

    loads[3].wait()
    loads[4].wait()
    for h in HALVES:
        span = slice(h, h + 128)
        s = csolid[PAD : PAD + C, span]
        f = collide([coarse[i, PAD : PAD + C, span] for i in range(19)], s, tau_coarse)
        for k in range(5):
            cto_left[k : k + 1, span] = f[LEFT[k]][0:1]
            cto_right[k : k + 1, span] = f[RIGHT[k]][C - 1 : C]
        cto_left[5:6, span] = s[0:1]
        cto_right[5:6, span] = s[C - 1 : C]
    chalo_r = pltpu.make_async_remote_copy(
        cto_right, cfrom_left, chalo_send.at[0], chalo_recv.at[0], right, MESH)
    chalo_r.start()

    row = lax.broadcasted_iota(jnp.int32, (256, 128), 0)
    column = lax.broadcasted_iota(jnp.int32, (256, 128), 1)
    hit = (row // 32 == column // 16) & ((row % 16) // 2 == column % 8)
    boxes[...] = jnp.where(hit, 0.125, 0.0).astype(jnp.bfloat16)

    def second_collision(start, rows):
        low, high = streamed(first, start, rows)
        for f, h in ((low, 0), (high, 128)):
            span = slice(h, h + 128)
            f = collide(f, solid[start : start + rows, span], tau_fine)
            for i in range(19):
                second[i, start : start + rows, span] = f[i]

    def box_means(pair_sums):
        rest, parts = pair_sums, []
        for _ in range(3):
            piece = rest.astype(jnp.bfloat16).astype(F32)
            parts.append(piece)
            rest = rest - piece
        stacked = jnp.concatenate(parts, axis=0).astype(jnp.bfloat16)
        product = jnp.dot(stacked, boxes[...], preferred_element_type=F32)
        n = pair_sums.shape[0]
        return product[:n] + product[n : 2 * n] + product[2 * n :]

    def rescaled(means, rows):
        a = jnp.full((rows, 128), 1.0 - rescale, F32)
        keep = jnp.full((rows, 128), 0.5 * rescale, F32)
        return relaxed([means[rows * i : rows * i + rows] for i in range(19)], keep, keep, a)

    def near(rows):
        return lanes(rows) % 16 < 8

    def deliver(which, buffer):
        sends = []
        for d, peer in enumerate(peers):
            sends.append(pltpu.make_async_remote_copy(
                buffer.at[g], buffer.at[g], box_send.at[which, d], box_recv.at[which, g],
                peer, MESH))
        for send in sends:
            send.start()
        return sends

    def collect(which, buffer):
        for d, peer in enumerate(peers):
            pltpu.make_async_remote_copy(
                buffer.at[peer[0]], buffer.at[peer[0]], box_send.at[which, d],
                box_recv.at[which, peer[0]], peer, MESH).wait_recv()

    for t in range(X // 8):
        second_collision(PAD + 8 * t, 8)
    for t in range(X // 8):
        low, high = streamed(second, PAD + 8 * t, 8)
        for i in range(19):
            moved[0, X * i + 8 * t : X * i + 8 * t + 8, :] = low[i]
            moved[1, X * i + 8 * t : X * i + 8 * t + 8, :] = high[i]
    sums = [
        moved[k, pl.ds(0, 152, stride=2), :] + moved[k, pl.ds(1, 152, stride=2), :]
        for k in range(2)
    ]
    f = rescaled(box_means(jnp.concatenate(sums, axis=1)), 8)
    for k in range(10):
        inner[g, k] = jnp.where(near(8), f[2 * k], f[min(2 * k + 1, 18)])
    sends = deliver(0, inner)

    pl.semaphore_wait(ready, 1)
    halo_l = pltpu.make_async_remote_copy(
        to_left, from_right, halo_send.at[1], halo_recv.at[1], left, MESH)
    halo_l.start()
    chalo_l = pltpu.make_async_remote_copy(
        cto_left, cfrom_right, chalo_send.at[1], chalo_recv.at[1], left, MESH)
    chalo_l.start()

    def outer_planes(side, outer):
        if side:
            low, high = streamed(second, PAD + X - 2, 4)
        else:
            low, high = streamed(second, PAD - 2, 4)
        for k, values in enumerate((low, high)):
            for i in range(19):
                edge[side, k, 4 * i : 4 * i + 4, :] = values[i]
                if side:
                    moved[k, X * i + X - 2 : X * i + X, :] = values[i][0:2]
                else:
                    moved[k, X * i : X * i + 2, :] = values[i][2:4]
        sums = [
            edge[side, k, pl.ds(0, 40, stride=2), :] + edge[side, k, pl.ds(1, 40, stride=2), :]
            for k in range(2)
        ]
        f = rescaled(box_means(jnp.concatenate(sums, axis=1)), 2)
        for k in range(10):
            outer[g, 2 * k : 2 * k + 2, :] = jnp.where(near(2), f[2 * k], f[min(2 * k + 1, 18)])

    halo_l.wait_recv()
    top = PAD + X
    for k, i in enumerate(LEFT + STAY):
        first[i, top : top + 4, :] = from_right[4 * k : 4 * k + 4, :]
    for k, i in enumerate(RIGHT):
        first[i, top : top + 2, :] = from_right[60 + 2 * k : 62 + 2 * k, :]
    solid[top : top + 4, :] = from_right[56:60, :]
    second_collision(top - 1, 4)
    outer_planes(1, outer_r)
    sends += deliver(1, outer_r)

    halo_r.wait_recv()
    for k, i in enumerate(RIGHT + STAY):
        first[i, PAD - 4 : PAD, :] = from_left[4 * k : 4 * k + 4, :]
    for k, i in enumerate(LEFT):
        first[i, PAD - 2 : PAD, :] = from_left[60 + 2 * k : 62 + 2 * k, :]
    solid[PAD - 4 : PAD, :] = from_left[56:60, :]
    second_collision(PAD - 3, 4)
    outer_planes(0, outer_l)
    sends += deliver(2, outer_l)

    sources, present = [], []
    for q in range(4):
        source = jnp.int32(0)
        found = jnp.int32(0)
        for k in range(groups):
            match = (slot_ref[k] == 4 * g + q).astype(jnp.int32)
            source = jnp.maximum(source, k * match)
            found = jnp.maximum(found, match)
        sources.append(source)
        present.append(found)

    def pasted(half, rows, tile, start):
        span = slice(128 * half, 128 * half + 128)
        one, two = sources[2 * half], sources[2 * half + 1]
        close = near(rows)
        put = jnp.where(
            close,
            jnp.full((rows, 128), present[2 * half], jnp.int32),
            jnp.full((rows, 128), present[2 * half + 1], jnp.int32),
        ) > 0
        f = []
        for k in range(10):
            tile_one, tile_two = tile(one, k), tile(two, k)
            i = 2 * k
            value = jnp.where(close, tile_one, pltpu.roll(tile_two, 8, 1))
            f.append(jnp.where(put, value, coarse[i, start : start + rows, span]))
            if i + 1 < 19:
                value = jnp.where(close, pltpu.roll(tile_one, 120, 1), tile_two)
                f.append(jnp.where(put, value, coarse[i + 1, start : start + rows, span]))
        return collide(f, csolid[start : start + rows, span], tau_coarse), put, span

    collect(0, inner)
    for half in range(2):
        f, _, span = pasted(half, C, lambda source, k: inner[source, k], PAD)
        for i in range(19):
            settled[i, PAD : PAD + C, span] = f[i]

    chalo_l.wait_recv()
    csolid[PAD + C : PAD + C + 1, :] = cfrom_right[5:6, :]
    collect(1, outer_r)
    for half in range(2):
        f, put, span = pasted(
            half, 2, lambda source, k: outer_r[source, 2 * k : 2 * k + 2, :], PAD + C - 1)
        for i in range(19):
            settled[i, PAD + C - 1 : PAD + C, span] = f[i][0:1]
        for k, i in enumerate(LEFT):
            settled[i, PAD + C : PAD + C + 1, span] = jnp.where(
                put[1:2], f[i][1:2], cfrom_right[k : k + 1, span])

    chalo_r.wait_recv()
    csolid[PAD - 1 : PAD, :] = cfrom_left[5:6, :]
    collect(2, outer_l)
    for half in range(2):
        f, put, span = pasted(
            half, 2, lambda source, k: outer_l[source, 2 * k : 2 * k + 2, :], PAD - 1)
        for i in range(19):
            settled[i, PAD : PAD + 1, span] = f[i][1:2]
        for k, i in enumerate(RIGHT):
            settled[i, PAD - 1 : PAD, span] = jnp.where(
                put[0:1], f[i][0:1], cfrom_left[k : k + 1, span])

    for copy in [halo_r, halo_l, chalo_r, chalo_l] + sends:
        copy.wait_send()


def finish(moved, settled, fine_out, coarse_out, cmoved, store_sem):
    stores = [
        pltpu.make_async_copy(moved.at[k], fine_out.at[0, :, :, h : h + 128], store_sem.at[k])
        for k, h in enumerate(HALVES)
    ]
    for store in stores:
        store.start()
    low, high = streamed(settled, PAD, C)
    for i in range(19):
        cmoved[i, :, 0:128] = low[i]
        cmoved[i, :, 128:256] = high[i]
    stores.append(pltpu.make_async_copy(cmoved, coarse_out.at[0], store_sem.at[2]))
    stores[2].start()
    for store in stores:
        store.wait()


def solution(mesh):
    groups, blocks = mesh.shape["grp"], mesh.shape["blk"]
    vmem = pl.BlockSpec(memory_space=pltpu.VMEM)
    hbm = pl.BlockSpec(memory_space=pltpu.HBM)

    def per_device(fine_pops, fine_solid, coarse_pops, coarse_solid, coarse_slot):
        body = lambda *refs: kernel(groups, blocks, *refs)
        moved, settled = pl.pallas_call(
            body,
            out_shape=(
                jax.ShapeDtypeStruct((2, 19 * X, 128), F32),
                jax.ShapeDtypeStruct((19, C + 2 * PAD, 256), F32),
            ),
            in_specs=[pl.BlockSpec(memory_space=pltpu.SMEM)] + [hbm] * 4,
            out_specs=(vmem, vmem),
            scratch_shapes=[
                pltpu.VMEM((19, X, 256), F32),
                pltpu.VMEM((X + 2 * PAD, 256), F32),
                pltpu.VMEM((19, C + 2 * PAD, 256), F32),
                pltpu.VMEM((C + 2 * PAD, 256), F32),
                pltpu.VMEM((19, X + 2 * PAD, 256), F32),
                pltpu.VMEM((19, X + 2 * PAD, 256), F32),
                pltpu.VMEM((2, 2, 80, 128), F32),
                pltpu.VMEM((256, 128), jnp.bfloat16),
                pltpu.VMEM((groups, 10, 8, 128), F32),
                pltpu.VMEM((groups, 24, 128), F32),
                pltpu.VMEM((groups, 24, 128), F32),
            ]
            + [pltpu.VMEM((72, 256), F32)] * 4
            + [pltpu.VMEM((8, 256), F32)] * 4
            + [
                pltpu.SemaphoreType.DMA((5,)),
                pltpu.SemaphoreType.REGULAR,
                pltpu.SemaphoreType.DMA((2,)),
                pltpu.SemaphoreType.DMA((2,)),
                pltpu.SemaphoreType.DMA((2,)),
                pltpu.SemaphoreType.DMA((2,)),
                pltpu.SemaphoreType.DMA((3, groups)),
                pltpu.SemaphoreType.DMA((3, groups)),
            ],
            compiler_params=pltpu.CompilerParams(
                collective_id=0, has_side_effects=True, vmem_limit_bytes=16 << 20),
        )(coarse_slot, *[
            pltpu.with_memory_space_constraint(x, pltpu.HBM)
            for x in (fine_pops, fine_solid, coarse_pops, coarse_solid)
        ])
        return pl.pallas_call(
            finish,
            out_shape=(
                jax.ShapeDtypeStruct(fine_pops.shape, F32),
                jax.ShapeDtypeStruct(coarse_pops.shape, F32),
            ),
            in_specs=[vmem, vmem],
            out_specs=(hbm, hbm),
            scratch_shapes=[pltpu.VMEM((19, C, 256), F32), pltpu.SemaphoreType.DMA((3,))],
            compiler_params=pltpu.CompilerParams(vmem_limit_bytes=4 << 20),
        )(moved.reshape(2, 19, X, 128), settled)

    placed = (
        P("grp", None, "blk", None),
        P("grp", "blk", None),
        P("grp", None, "blk", None),
        P("grp", "blk", None),
        P(),
    )
    return jax.shard_map(
        per_device,
        mesh=mesh,
        in_specs=placed,
        out_specs=(P("grp", None, "blk", None), P("grp", None, "blk", None)),
        check_vma=False,
    )
```

time: 37.2 us -> 30.1 us (0.81)
  Pallas kernels: 33.9 us -> 28.6 us
  local copies, waits for them, and re-layouts: 2.41 us -> 0.65 us
    pallas_call x1 -> x2, Pallas kernels: 33.9 us -> 28.6 us  [the longest x1 27.8 us: per_device(): pl.pallas_call(body, out_shape=(jax.ShapeDtypeStruct((2, 19 * X, 128), F3...]
    unnamed x4 -> x2, local copies, waits for them, and re-layouts: 2.41 us -> 0.65 us
where the time goes in v2:
time: 30.1 us; the launch traced here: 29.9 us
  Pallas kernels  28.6 us (95%)
  local copies, waits for them, and re-layouts  0.65 us (2%)
  between operations  0.65 us (2%)
    pallas_call x1, Pallas kernels, per_device(): pl.pallas_call(body, out_shape=(jax.ShapeDtypeStruct((2, 19 * X, 128), F3...  27.8 us
    pallas_call x1, Pallas kernels, per_device(): pl.pallas_call(finish, out_shape=(jax.ShapeDtypeStruct(fine_pops.shape, F...  0.81 us
    unnamed x2, local copies, waits for them, and re-layouts  0.65 us

profile of v2, /device:TPU:1, one launch (start us, length us, event | category | flops | bytes accessed | tf_op | source)
XLA Modules:
  0.0 29.9 jit_solution(4996585800811595683)
XLA Ops:
  0.6 0.0 copy-start
  0.6 0.6 %copy-done = s32[8]{0:T(128)S(1)} copy-done((s32[8]{0:T(128)S(1)}, s32[8]{0:T(128)}, u32[]{:S(2)}) %copy-start) | copy-done | bytes 56
  1.3 27.8 %shard_map.68 = (f32[2,304,128]{2,1,0:T(8,128)S(1)}, f32[19,24,256]{2,1,0:T(8,128)S(1)}) custom-call(s32[8]{0:T(128)S(1)} %copy-done, f32[1,19,16,256]{3,2,1,0:T(8,128)} %refs_1_.1, f32[1,16,256]{2,1,0:T(8,128)} %refs_2_.1, f32[1,19,8,256]{3,2,1,0:T(8,128)} %refs_3_.1, f32[1,8,256]{2,1,0:T(8,128)} %refs_4_.1), custom_call_target="tpu_custom_call" | custom-call | tf_op jit(solution)/shard_map/pallas_call | solution.py:401
  29.1 0.8 %shard_map.69 = (f32[1,19,16,256]{3,2,1,0:T(8,128)}, f32[1,19,8,256]{3,2,1,0:T(8,128)}) custom-call(f32[2,19,16,128]{3,2,1,0:T(8,128)S(1)} %bitcast.1, f32[19,24,256]{2,1,0:T(8,128)S(1)} %get-tuple-element.5.settled), custom_call_target="tpu_custom_call" | custom-call | tf_op jit(solution)/shard_map/pallas_call | solution.py:440
Async XLA Ops:
  0.6 0.7 %copy-start = (s32[8]{0:T(128)S(1)}, s32[8]{0:T(128)}, u32[]{:S(2)}) copy-start(s32[8]{0:T(128)} %refs_0_.1) | copy-start | bytes 100

commit v3 on v2

--- a/solution.py
+++ b/solution.py
@@ -22,6 +22,7 @@
 STAY = [i for i in range(19) if lattice_vel[i][0] == 0]
 X = 16
 C = 8
+ROW = 12
 PAD = 8
 HALVES = (0, 128)
 
@@ -122,10 +123,11 @@
 
 
 def kernel(
-    groups, blocks, slot_ref, fine_hbm, solid_hbm, coarse_hbm, csolid_hbm, moved, settled,
+    groups, blocks, slot_hbm, fine_hbm, solid_hbm, coarse_hbm, csolid_hbm,
+    fine_view, solid_view, coarse_view, csolid_view, moved, settled,
     fine, solid, coarse, csolid, first, second, edge, boxes, inner, outer_r, outer_l,
-    to_right, to_left, from_left, from_right, cto_right, cto_left, cfrom_left, cfrom_right,
-    load_sem, ready, halo_send, halo_recv, chalo_send, chalo_recv, box_send, box_recv,
+    from_left, from_right, sol_left, sol_right, cfrom_left, cfrom_right, csol_left, csol_right,
+    slot_ref, load_sem, ready, lefts, peers_in, halo_send, halo_recv, box_send, box_recv,
 ):
     g = lax.axis_index("grp")
     b = lax.axis_index("blk")
@@ -133,68 +135,52 @@
     left = (g, lax.rem(b + blocks - 1, blocks))
     peers = [(lax.rem(g + d, groups), b) for d in (4, 3, 5, 2, 6, 1, 7)]
 
+    late = lax.rem(b, ROW) == ROW - 1
+    follows = lax.rem(b, ROW) == 0
+
+    barrier = pltpu.get_barrier_semaphore()
+    pl.semaphore_signal(barrier, inc=1, device_id=left, device_id_type=MESH)
+
+    @pl.when(jnp.logical_not(late))
+    def _():
+        for device in peers:
+            pl.semaphore_signal(barrier, inc=1, device_id=device, device_id_type=MESH)
+
     loads = [
         pltpu.make_async_copy(solid_hbm.at[0], solid.at[PAD : PAD + X], load_sem.at[0]),
-        pltpu.make_async_copy(fine_hbm.at[0, :, 8:16], fine.at[:, 8:16], load_sem.at[1]),
-        pltpu.make_async_copy(fine_hbm.at[0, :, 0:8], fine.at[:, 0:8], load_sem.at[2]),
-        pltpu.make_async_copy(csolid_hbm.at[0], csolid.at[PAD : PAD + C], load_sem.at[3]),
-        pltpu.make_async_copy(coarse_hbm.at[0], coarse.at[:, PAD : PAD + C], load_sem.at[4]),
+        pltpu.make_async_copy(fine_hbm.at[0], fine, load_sem.at[1]),
+        pltpu.make_async_copy(csolid_hbm.at[0], csolid.at[PAD : PAD + C], load_sem.at[2]),
+        pltpu.make_async_copy(coarse_hbm.at[0], coarse.at[:, PAD : PAD + C], load_sem.at[3]),
+        pltpu.make_async_copy(slot_hbm, slot_ref, load_sem.at[4]),
     ]
+
+    def halo(k, source, target, device):
+        return pltpu.make_async_remote_copy(
+            source, target, halo_send.at[k], halo_recv.at[k], device, MESH)
+
+    halos_r = [
+        halo(0, fine_view.at[:, 1, :, 4:8], from_left, right),
+        halo(1, solid_view.at[1, :, 4:8], sol_left, right),
+        halo(2, coarse_view.at[:, :, C - 1 : C], cfrom_left, right),
+        halo(3, csolid_view.at[:, C - 1 : C], csol_left, right),
+    ]
+    halos_l = [
+        halo(4, fine_view.at[:, 0, :, 0:4], from_right, left),
+        halo(5, solid_view.at[0, :, 0:4], sol_right, left),
+        halo(6, coarse_view.at[:, :, 0:1], cfrom_right, left),
+        halo(7, csolid_view.at[:, 0:1], csol_right, left),
+    ]
+    pl.semaphore_wait(barrier, jnp.where(late, 1, groups))
+    for copy in halos_r:
+        copy.start()
+    pl.semaphore_signal(ready, inc=1, device_id=right, device_id_type=MESH)
     for load in loads:
         load.start()
-    barrier = pltpu.get_barrier_semaphore()
-    for device in [left] + peers:
-        pl.semaphore_signal(barrier, inc=1, device_id=device, device_id_type=MESH)
-
-    def first_collision(t):
-        out = []
-        for h in HALVES:
-            span = slice(h, h + 128)
-            f = [fine[i, 8 * t : 8 * t + 8, span] for i in range(19)]
-            f = collide(f, solid[PAD + 8 * t : PAD + 8 * t + 8, span], tau_fine)
-            for i in range(19):
-                first[i, PAD + 8 * t : PAD + 8 * t + 8, span] = f[i]
-            out.append(f)
-        return out
-
-    loads[0].wait()
-    loads[1].wait()
-    for f, h in zip(first_collision(1), HALVES):
-        span = slice(h, h + 128)
-        for k, i in enumerate(RIGHT + STAY):
-            to_right[4 * k : 4 * k + 4, span] = f[i][4:8]
-        to_right[56:60, span] = solid[PAD + 12 : PAD + 16, span]
-        for k, i in enumerate(LEFT):
-            to_right[60 + 2 * k : 62 + 2 * k, span] = f[i][6:8]
-    pl.semaphore_wait(barrier, groups)
-    halo_r = pltpu.make_async_remote_copy(
-        to_right, from_left, halo_send.at[0], halo_recv.at[0], right, MESH)
-    halo_r.start()
-    pl.semaphore_signal(ready, inc=1, device_id=right, device_id_type=MESH)
-
-    loads[2].wait()
-    for f, h in zip(first_collision(0), HALVES):
-        span = slice(h, h + 128)
-        for k, i in enumerate(LEFT + STAY):
-            to_left[4 * k : 4 * k + 4, span] = f[i][0:4]
-        to_left[56:60, span] = solid[PAD : PAD + 4, span]
-        for k, i in enumerate(RIGHT):
-            to_left[60 + 2 * k : 62 + 2 * k, span] = f[i][0:2]
-
-    loads[3].wait()
-    loads[4].wait()
-    for h in HALVES:
-        span = slice(h, h + 128)
-        s = csolid[PAD : PAD + C, span]
-        f = collide([coarse[i, PAD : PAD + C, span] for i in range(19)], s, tau_coarse)
-        for k in range(5):
-            cto_left[k : k + 1, span] = f[LEFT[k]][0:1]
-            cto_right[k : k + 1, span] = f[RIGHT[k]][C - 1 : C]
-        cto_left[5:6, span] = s[0:1]
-        cto_right[5:6, span] = s[C - 1 : C]
-    chalo_r = pltpu.make_async_remote_copy(
-        cto_right, cfrom_left, chalo_send.at[0], chalo_recv.at[0], right, MESH)
-    chalo_r.start()
+
+    def first_collision(f, s, start, rows, span):
+        f = collide(f, s, tau_fine)
+        for i in range(19):
+            first[i, start : start + rows, span] = f[i]
 
     row = lax.broadcasted_iota(jnp.int32, (256, 128), 0)
     column = lax.broadcasted_iota(jnp.int32, (256, 128), 1)
@@ -228,15 +214,19 @@
     def near(rows):
         return lanes(rows) % 16 < 8
 
-    def deliver(which, buffer):
-        sends = []
-        for d, peer in enumerate(peers):
-            sends.append(pltpu.make_async_remote_copy(
+    def messages(which, buffer):
+        return [
+            pltpu.make_async_remote_copy(
                 buffer.at[g], buffer.at[g], box_send.at[which, d], box_recv.at[which, g],
-                peer, MESH))
-        for send in sends:
+                peer, MESH)
+            for d, peer in enumerate(peers)
+        ]
+
+    sends = [messages(0, inner), messages(1, outer_r), messages(2, outer_l)]
+
+    def deliver(which):
+        for send in sends[which]:
             send.start()
-        return sends
 
     def collect(which, buffer):
         for d, peer in enumerate(peers):
@@ -244,6 +234,14 @@
                 buffer.at[peer[0]], buffer.at[peer[0]], box_send.at[which, d],
                 box_recv.at[which, peer[0]], peer, MESH).wait_recv()
 
+    loads[0].wait()
+    loads[1].wait()
+    for t in range(X // 8):
+        for h in HALVES:
+            span = slice(h, h + 128)
+            first_collision(
+                [fine[i, 8 * t : 8 * t + 8, span] for i in range(19)],
+                solid[PAD + 8 * t : PAD + 8 * t + 8, span], PAD + 8 * t, 8, span)
     for t in range(X // 8):
         second_collision(PAD + 8 * t, 8)
     for t in range(X // 8):
@@ -258,15 +256,26 @@
     f = rescaled(box_means(jnp.concatenate(sums, axis=1)), 8)
     for k in range(10):
         inner[g, k] = jnp.where(near(8), f[2 * k], f[min(2 * k + 1, 18)])
-    sends = deliver(0, inner)
+
+    @pl.when(jnp.logical_not(late))
+    def _():
+        deliver(0)
 
     pl.semaphore_wait(ready, 1)
-    halo_l = pltpu.make_async_remote_copy(
-        to_left, from_right, halo_send.at[1], halo_recv.at[1], left, MESH)
-    halo_l.start()
-    chalo_l = pltpu.make_async_remote_copy(
-        cto_left, cfrom_right, chalo_send.at[1], chalo_recv.at[1], left, MESH)
-    chalo_l.start()
+    for copy in halos_l:
+        copy.start()
+
+    @pl.when(follows)
+    def _():
+        for device in peers:
+            pl.semaphore_signal(lefts, inc=1, device_id=device, device_id_type=MESH)
+
+    def beyond(halo, halo_solid, start):
+        for k, h in enumerate(HALVES):
+            span = slice(h, h + 128)
+            s = halo_solid[k, :, 0, :]
+            solid[start : start + 4, span] = s
+            first_collision([halo[i, k, :, 0, :] for i in range(19)], s, start, 4, span)
 
     def outer_planes(side, outer):
         if side:
@@ -288,27 +297,36 @@
         for k in range(10):
             outer[g, 2 * k : 2 * k + 2, :] = jnp.where(near(2), f[2 * k], f[min(2 * k + 1, 18)])
 
-    halo_l.wait_recv()
-    top = PAD + X
-    for k, i in enumerate(LEFT + STAY):
-        first[i, top : top + 4, :] = from_right[4 * k : 4 * k + 4, :]
-    for k, i in enumerate(RIGHT):
-        first[i, top : top + 2, :] = from_right[60 + 2 * k : 62 + 2 * k, :]
-    solid[top : top + 4, :] = from_right[56:60, :]
-    second_collision(top - 1, 4)
+    halos_l[0].wait_recv()
+    halos_l[1].wait_recv()
+    beyond(from_right, sol_right, PAD + X)
+    second_collision(PAD + X - 1, 4)
     outer_planes(1, outer_r)
-    sends += deliver(1, outer_r)
-
-    halo_r.wait_recv()
-    for k, i in enumerate(RIGHT + STAY):
-        first[i, PAD - 4 : PAD, :] = from_left[4 * k : 4 * k + 4, :]
-    for k, i in enumerate(LEFT):
-        first[i, PAD - 2 : PAD, :] = from_left[60 + 2 * k : 62 + 2 * k, :]
-    solid[PAD - 4 : PAD, :] = from_left[56:60, :]
+
+    @pl.when(jnp.logical_not(late))
+    def _():
+        deliver(1)
+
+    @pl.when(follows)
+    def _():
+        pl.semaphore_wait(lefts, groups - 1)
+        pl.semaphore_signal(peers_in, inc=1, device_id=left, device_id_type=MESH)
+
+    halos_r[0].wait_recv()
+    halos_r[1].wait_recv()
+    beyond(from_left, sol_left, PAD - 4)
     second_collision(PAD - 3, 4)
     outer_planes(0, outer_l)
-    sends += deliver(2, outer_l)
-
+
+    @pl.when(late)
+    def _():
+        pl.semaphore_wait(peers_in, 1)
+        deliver(0)
+        deliver(1)
+
+    deliver(2)
+
+    loads[4].wait()
     sources, present = [], []
     for q in range(4):
         source = jnp.int32(0)
@@ -338,39 +356,44 @@
             if i + 1 < 19:
                 value = jnp.where(close, pltpu.roll(tile_one, 120, 1), tile_two)
                 f.append(jnp.where(put, value, coarse[i + 1, start : start + rows, span]))
-        return collide(f, csolid[start : start + rows, span], tau_coarse), put, span
-
+        return collide(f, csolid[start : start + rows, span], tau_coarse), span
+
+    def cbeyond(halo, halo_solid, start):
+        for k, h in enumerate(HALVES):
+            span = slice(h, h + 128)
+            csolid[start : start + 1, span] = halo_solid[k, :, 0, :]
+            for i in range(19):
+                coarse[i, start : start + 1, span] = halo[i, k, :, 0, :]
+
+    loads[2].wait()
+    loads[3].wait()
+    halos_l[2].wait_recv()
+    halos_l[3].wait_recv()
+    cbeyond(cfrom_right, csol_right, PAD + C)
     collect(0, inner)
     for half in range(2):
-        f, _, span = pasted(half, C, lambda source, k: inner[source, k], PAD)
+        f, span = pasted(half, C, lambda source, k: inner[source, k], PAD)
         for i in range(19):
             settled[i, PAD : PAD + C, span] = f[i]
 
-    chalo_l.wait_recv()
-    csolid[PAD + C : PAD + C + 1, :] = cfrom_right[5:6, :]
     collect(1, outer_r)
     for half in range(2):
-        f, put, span = pasted(
+        f, span = pasted(
             half, 2, lambda source, k: outer_r[source, 2 * k : 2 * k + 2, :], PAD + C - 1)
         for i in range(19):
-            settled[i, PAD + C - 1 : PAD + C, span] = f[i][0:1]
-        for k, i in enumerate(LEFT):
-            settled[i, PAD + C : PAD + C + 1, span] = jnp.where(
-                put[1:2], f[i][1:2], cfrom_right[k : k + 1, span])
-
-    chalo_r.wait_recv()
-    csolid[PAD - 1 : PAD, :] = cfrom_left[5:6, :]
+            settled[i, PAD + C - 1 : PAD + C + 1, span] = f[i]
+
+    halos_r[2].wait_recv()
+    halos_r[3].wait_recv()
+    cbeyond(cfrom_left, csol_left, PAD - 1)
     collect(2, outer_l)
     for half in range(2):
-        f, put, span = pasted(
+        f, span = pasted(
             half, 2, lambda source, k: outer_l[source, 2 * k : 2 * k + 2, :], PAD - 1)
         for i in range(19):
-            settled[i, PAD : PAD + 1, span] = f[i][1:2]
-        for k, i in enumerate(RIGHT):
-            settled[i, PAD - 1 : PAD, span] = jnp.where(
-                put[0:1], f[i][0:1], cfrom_left[k : k + 1, span])
-
-    for copy in [halo_r, halo_l, chalo_r, chalo_l] + sends:
+            settled[i, PAD - 1 : PAD + 1, span] = f[i]
+
+    for copy in halos_r + halos_l + sends[0] + sends[1] + sends[2]:
         copy.wait_send()
 
 
@@ -396,6 +419,12 @@
     vmem = pl.BlockSpec(memory_space=pltpu.VMEM)
     hbm = pl.BlockSpec(memory_space=pltpu.HBM)
 
+    def planes(x, *leading):
+        n = len(leading)
+        order = tuple(range(n)) + (n + 1, n, n + 2)
+        x = x.reshape(leading + (8, 2, 128)).transpose(order)
+        return x.reshape(leading + (2, 8, 1, 128))
+
     def per_device(fine_pops, fine_solid, coarse_pops, coarse_solid, coarse_slot):
         body = lambda *refs: kernel(groups, blocks, *refs)
         moved, settled = pl.pallas_call(
@@ -404,7 +433,7 @@
                 jax.ShapeDtypeStruct((2, 19 * X, 128), F32),
                 jax.ShapeDtypeStruct((19, C + 2 * PAD, 256), F32),
             ),
-            in_specs=[pl.BlockSpec(memory_space=pltpu.SMEM)] + [hbm] * 4,
+            in_specs=[hbm] * 9,
             out_specs=(vmem, vmem),
             scratch_shapes=[
                 pltpu.VMEM((19, X, 256), F32),
@@ -419,23 +448,30 @@
                 pltpu.VMEM((groups, 24, 128), F32),
                 pltpu.VMEM((groups, 24, 128), F32),
             ]
-            + [pltpu.VMEM((72, 256), F32)] * 4
-            + [pltpu.VMEM((8, 256), F32)] * 4
+            + [pltpu.VMEM((19, 2, 4, 1, 128), F32)] * 2
+            + [pltpu.VMEM((2, 4, 1, 128), F32)] * 2
+            + [pltpu.VMEM((19, 2, 1, 1, 128), F32)] * 2
+            + [pltpu.VMEM((2, 1, 1, 128), F32)] * 2
             + [
+                pltpu.SMEM((groups,), jnp.int32),
                 pltpu.SemaphoreType.DMA((5,)),
                 pltpu.SemaphoreType.REGULAR,
-                pltpu.SemaphoreType.DMA((2,)),
-                pltpu.SemaphoreType.DMA((2,)),
-                pltpu.SemaphoreType.DMA((2,)),
-                pltpu.SemaphoreType.DMA((2,)),
+                pltpu.SemaphoreType.REGULAR,
+                pltpu.SemaphoreType.REGULAR,
+                pltpu.SemaphoreType.DMA((8,)),
+                pltpu.SemaphoreType.DMA((8,)),
                 pltpu.SemaphoreType.DMA((3, groups)),
                 pltpu.SemaphoreType.DMA((3, groups)),
             ],
             compiler_params=pltpu.CompilerParams(
                 collective_id=0, has_side_effects=True, vmem_limit_bytes=16 << 20),
-        )(coarse_slot, *[
+        )(*[
             pltpu.with_memory_space_constraint(x, pltpu.HBM)
-            for x in (fine_pops, fine_solid, coarse_pops, coarse_solid)
+            for x in (
+                coarse_slot, fine_pops, fine_solid, coarse_pops, coarse_solid,
+                planes(fine_pops, 19, 2), planes(fine_solid, 2),
+                planes(coarse_pops, 19), planes(coarse_solid),
+            )
         ])
         return pl.pallas_call(
             finish,

time: 30.1 us -> 28.3 us (0.940)
  Pallas kernels: 28.6 us -> 27.4 us
  local copies, waits for them, and re-layouts: 0.65 us -> 0 us
    pallas_call x1, Pallas kernels: 27.8 us -> 26.6 us  [per_device(): pl.pallas_call(body, out_shape=(jax.ShapeDtypeStruct((2, 19 * X, 128), F3...]
    unnamed x2 -> x0, local copies, waits for them, and re-layouts: 0.65 us -> none
where the time goes in v3:
time: 28.3 us; the launch traced here: 28.1 us
  Pallas kernels  27.4 us (97%)
  between operations  0.64 us (2%)
    pallas_call x1, Pallas kernels, per_device(): pl.pallas_call(body, out_shape=(jax.ShapeDtypeStruct((2, 19 * X, 128), F3...  26.6 us
    pallas_call x1, Pallas kernels, per_device(): pl.pallas_call(finish, out_shape=(jax.ShapeDtypeStruct(fine_pops.shape, F...  0.81 us

profile of v3, /device:TPU:1, one launch (start us, length us, event | category | flops | bytes accessed | tf_op | source)
XLA Modules:
  0.0 28.1 jit_solution(9161422577192498090)
XLA Ops:
  0.6 26.6 %shard_map.68 = (f32[2,304,128]{2,1,0:T(8,128)S(1)}, f32[19,24,256]{2,1,0:T(8,128)S(1)}) custom-call(s32[8]{0:T(128)} %refs_0_.1, f32[1,19,16,256]{3,2,1,0:T(8,128)} %refs_1_.1, f32[1,16,256]{2,1,0:T(8,128)} %refs_2_.1, f32[1,19,8,256]{3,2,1,0:T(8,128)} %refs_3_.1, f32[1,8,256]{2,1,0:T(8,128)} %refs_4_.1, f32[19,2,2,8,1,128]{5,4,3,2,1,0:T(1,128)} %bitcast.22, ...), custom_call_target="tpu_custom_call" | custom-call | tf_op jit(solution)/shard_map/pallas_call | solution.py:430
  27.3 0.8 %shard_map.69 = (f32[1,19,16,256]{3,2,1,0:T(8,128)}, f32[1,19,8,256]{3,2,1,0:T(8,128)}) custom-call(f32[2,19,16,128]{3,2,1,0:T(8,128)S(1)} %bitcast.21, f32[19,24,256]{2,1,0:T(8,128)S(1)} %get-tuple-element.5.settled), custom_call_target="tpu_custom_call" | custom-call | tf_op jit(solution)/shard_map/pallas_call | solution.py:476

commit v4 on v3

--- a/solution.py
+++ b/solution.py
@@ -133,7 +133,12 @@
     b = lax.axis_index("blk")
     right = (g, lax.rem(b + 1, blocks))
     left = (g, lax.rem(b + blocks - 1, blocks))
-    peers = [(lax.rem(g + d, groups), b) for d in (4, 3, 5, 2, 6, 1, 7)]
+    half = groups // 2
+    place = jnp.where(lax.rem(g, 2) == 1, g // 2, half + lax.rem(g // 2 + half - 1, half))
+    peers = []
+    for k in range(groups - 1):
+        k = k + (place <= k).astype(jnp.int32)
+        peers.append((jnp.where(k < half, 2 * k + 1, lax.rem(2 * (k - half) + 2, groups)), b))
 
     late = lax.rem(b, ROW) == ROW - 1
     follows = lax.rem(b, ROW) == 0
@@ -159,19 +164,19 @@
             source, target, halo_send.at[k], halo_recv.at[k], device, MESH)
 
     halos_r = [
-        halo(0, fine_view.at[:, 1, :, 4:8], from_left, right),
-        halo(1, solid_view.at[1, :, 4:8], sol_left, right),
+        halo(0, solid_view.at[1, :, 4:8], sol_left, right),
+        halo(1, fine_view.at[:, 1, :, 4:8], from_left, right),
         halo(2, coarse_view.at[:, :, C - 1 : C], cfrom_left, right),
         halo(3, csolid_view.at[:, C - 1 : C], csol_left, right),
     ]
     halos_l = [
-        halo(4, fine_view.at[:, 0, :, 0:4], from_right, left),
-        halo(5, solid_view.at[0, :, 0:4], sol_right, left),
+        halo(4, solid_view.at[0, :, 0:4], sol_right, left),
+        halo(5, fine_view.at[:, 0, :, 0:4], from_right, left),
         halo(6, coarse_view.at[:, :, 0:1], cfrom_right, left),
         halo(7, csolid_view.at[:, 0:1], csol_right, left),
     ]
     pl.semaphore_wait(barrier, jnp.where(late, 1, groups))
-    for copy in halos_r:
+    for copy in halos_r[:2]:
         copy.start()
     pl.semaphore_signal(ready, inc=1, device_id=right, device_id_type=MESH)
     for load in loads:
@@ -260,6 +265,9 @@
     @pl.when(jnp.logical_not(late))
     def _():
         deliver(0)
+
+    for copy in halos_r[2:]:
+        copy.start()
 
     pl.semaphore_wait(ready, 1)
     for copy in halos_l:

time: 28.3 us -> 27.8 us (0.982)
  Pallas kernels: 27.4 us -> 26.9 us
    pallas_call x1, Pallas kernels: 26.6 us -> 26.1 us  [per_device(): pl.pallas_call(body, out_shape=(jax.ShapeDtypeStruct((2, 19 * X, 128), F3...]
where the time goes in v4:
time: 27.8 us; the launch traced here: 27.6 us
  Pallas kernels  26.9 us (97%)
  between operations  0.64 us (2%)
    pallas_call x1, Pallas kernels, per_device(): pl.pallas_call(body, out_shape=(jax.ShapeDtypeStruct((2, 19 * X, 128), F3...  26.1 us
    pallas_call x1, Pallas kernels, per_device(): pl.pallas_call(finish, out_shape=(jax.ShapeDtypeStruct(fine_pops.shape, F...  0.81 us

profile of v4, /device:TPU:1, one launch (start us, length us, event | category | flops | bytes accessed | tf_op | source)
XLA Modules:
  0.0 27.6 jit_solution(14004794198923718194)
XLA Ops:
  0.6 26.1 %shard_map.68 = (f32[2,304,128]{2,1,0:T(8,128)S(1)}, f32[19,24,256]{2,1,0:T(8,128)S(1)}) custom-call(s32[8]{0:T(128)} %refs_0_.1, f32[1,19,16,256]{3,2,1,0:T(8,128)} %refs_1_.1, f32[1,16,256]{2,1,0:T(8,128)} %refs_2_.1, f32[1,19,8,256]{3,2,1,0:T(8,128)} %refs_3_.1, f32[1,8,256]{2,1,0:T(8,128)} %refs_4_.1, f32[19,2,2,8,1,128]{5,4,3,2,1,0:T(1,128)} %bitcast.22, ...), custom_call_target="tpu_custom_call" | custom-call | tf_op jit(solution)/shard_map/pallas_call | solution.py:438
  26.7 0.8 %shard_map.69 = (f32[1,19,16,256]{3,2,1,0:T(8,128)}, f32[1,19,8,256]{3,2,1,0:T(8,128)}) custom-call(f32[2,19,16,128]{3,2,1,0:T(8,128)S(1)} %bitcast.21, f32[19,24,256]{2,1,0:T(8,128)S(1)} %get-tuple-element.5.settled), custom_call_target="tpu_custom_call" | custom-call | tf_op jit(solution)/shard_map/pallas_call | solution.py:484

commit v5 on v4

--- a/solution.py
+++ b/solution.py
@@ -27,27 +27,24 @@
 HALVES = (0, 128)
 
 
+def total(terms):
+    while len(terms) > 1:
+        terms = [a + b for a, b in zip(terms[::2], terms[1::2])] + terms[len(terms) // 2 * 2 :]
+    return terms[0]
+
+
 def relaxed(f, keep_even, keep_odd, a):
     even = [None] * 19
     odd = [None] * 19
     for i in range(1, 19, 2):
         even[i] = f[i] + f[i + 1]
         odd[i] = f[i] - f[i + 1]
-    rho = f[0]
-    for i in range(1, 19, 2):
-        rho = rho + even[i]
+    rho = total([f[0]] + [even[i] for i in range(1, 19, 2)])
     j = []
     for axis in range(3):
-        total = None
-        for i in range(1, 19, 2):
-            c = lattice_vel[i][axis]
-            if c:
-                term = odd[i]
-                if total is None:
-                    total = term if c > 0 else -term
-                else:
-                    total = total + term if c > 0 else total - term
-        j.append(total)
+        plus = [odd[i] for i in range(1, 19, 2) if lattice_vel[i][axis] > 0]
+        minus = [odd[i] for i in range(1, 19, 2) if lattice_vel[i][axis] < 0]
+        j.append(total(plus) - total(minus) if minus else total(plus))
     inverse = 1.0 / rho
     q = a * inverse
     jj = j[0] * j[0] + j[1] * j[1] + j[2] * j[2]
@@ -122,10 +119,32 @@
     return low, high
 
 
+def packed(source, row):
+    lane = lanes(8)
+    odd = lax.broadcasted_iota(jnp.int32, (8, 128), 0) % 2 == 1
+    out = []
+    for i in range(19):
+        cx, cy, cz = lattice_vel[i]
+        start = 16 * i + row - 2 * cx
+        v = source[start : start + 8, :]
+        if cy or cz:
+            shift = 16 * cy + cz
+            m = pltpu.roll(v, shift % 128, 1)
+            if cz:
+                wrapped = pltpu.roll(v, (shift - 16 * cz) % 128, 1)
+                m = jnp.where(lane % 16 == (0 if cz > 0 else 15), wrapped, m)
+            if cy:
+                other = jnp.where(odd, pltpu.roll(m, 1, 0), pltpu.roll(m, 7, 0))
+                m = jnp.where(lane < 16 if cy > 0 else lane >= 112, other, m)
+            v = m
+        out.append(v)
+    return out
+
+
 def kernel(
     groups, blocks, slot_hbm, fine_hbm, solid_hbm, coarse_hbm, csolid_hbm,
     fine_view, solid_view, coarse_view, csolid_view, moved, settled,
-    fine, solid, coarse, csolid, first, second, edge, boxes, inner, outer_r, outer_l,
+    fine, solid, coarse, csolid, first, second, edge, pfirst, psecond, psolid, pmoved, boxes, inner, outer_r, outer_l,
     from_left, from_right, sol_left, sol_right, cfrom_left, cfrom_right, csol_left, csol_right,
     slot_ref, load_sem, ready, lefts, peers_in, halo_send, halo_recv, box_send, box_recv,
 ):
@@ -247,8 +266,17 @@
             first_collision(
                 [fine[i, 8 * t : 8 * t + 8, span] for i in range(19)],
                 solid[PAD + 8 * t : PAD + 8 * t + 8, span], PAD + 8 * t, 8, span)
+    for k, h in enumerate(HALVES):
+        span = slice(h, h + 128)
+        psolid[pl.ds(8 + k, 4, stride=2), :] = solid[PAD : PAD + 4, span]
+        for i in range(19):
+            pfirst[pl.ds(16 * i + 8 + k, 4, stride=2), :] = first[i, PAD : PAD + 4, span]
     for t in range(X // 8):
         second_collision(PAD + 8 * t, 8)
+    for k, h in enumerate(HALVES):
+        for i in range(19):
+            psecond[pl.ds(16 * i + 10 + k, 2, stride=2), :] = second[
+                i, PAD + 1 : PAD + 3, h : h + 128]
     for t in range(X // 8):
         low, high = streamed(second, PAD + 8 * t, 8)
         for i in range(19):
@@ -285,22 +313,7 @@
             solid[start : start + 4, span] = s
             first_collision([halo[i, k, :, 0, :] for i in range(19)], s, start, 4, span)
 
-    def outer_planes(side, outer):
-        if side:
-            low, high = streamed(second, PAD + X - 2, 4)
-        else:
-            low, high = streamed(second, PAD - 2, 4)
-        for k, values in enumerate((low, high)):
-            for i in range(19):
-                edge[side, k, 4 * i : 4 * i + 4, :] = values[i]
-                if side:
-                    moved[k, X * i + X - 2 : X * i + X, :] = values[i][0:2]
-                else:
-                    moved[k, X * i : X * i + 2, :] = values[i][2:4]
-        sums = [
-            edge[side, k, pl.ds(0, 40, stride=2), :] + edge[side, k, pl.ds(1, 40, stride=2), :]
-            for k in range(2)
-        ]
+    def restricted(sums, outer):
         f = rescaled(box_means(jnp.concatenate(sums, axis=1)), 2)
         for k in range(10):
             outer[g, 2 * k : 2 * k + 2, :] = jnp.where(near(2), f[2 * k], f[min(2 * k + 1, 18)])
@@ -309,7 +322,14 @@
     halos_l[1].wait_recv()
     beyond(from_right, sol_right, PAD + X)
     second_collision(PAD + X - 1, 4)
-    outer_planes(1, outer_r)
+    low, high = streamed(second, PAD + X - 2, 4)
+    for k, values in enumerate((low, high)):
+        for i in range(19):
+            edge[k, 4 * i : 4 * i + 4, :] = values[i]
+            moved[k, X * i + X - 2 : X * i + X, :] = values[i][0:2]
+    restricted(
+        [edge[k, pl.ds(0, 40, stride=2), :] + edge[k, pl.ds(1, 40, stride=2), :] for k in range(2)],
+        outer_r)
 
     @pl.when(jnp.logical_not(late))
     def _():
@@ -322,9 +342,22 @@
 
     halos_r[0].wait_recv()
     halos_r[1].wait_recv()
-    beyond(from_left, sol_left, PAD - 4)
-    second_collision(PAD - 3, 4)
-    outer_planes(0, outer_l)
+    s = sol_left[...].reshape(8, 128)
+    f = collide([from_left[i].reshape(8, 128) for i in range(19)], s, tau_fine)
+    for k in range(2):
+        psolid[pl.ds(k, 4, stride=2), :] = s[4 * k : 4 * k + 4]
+        for i in range(19):
+            pfirst[pl.ds(16 * i + k, 4, stride=2), :] = f[i][4 * k : 4 * k + 4]
+    f = collide(packed(pfirst, 2), psolid[2:10, :], tau_fine)
+    for i in range(19):
+        psecond[16 * i + 2 : 16 * i + 10, :] = f[i]
+    f = packed(psecond, 4)
+    for i in range(19):
+        pmoved[8 * i : 8 * i + 8, :] = f[i]
+    restricted(
+        [pmoved[pl.ds(k, 40, stride=4), :] + pmoved[pl.ds(k + 2, 40, stride=4), :]
+         for k in range(2)],
+        outer_l)
 
     @pl.when(late)
     def _():
@@ -333,6 +366,9 @@
         deliver(1)
 
     deliver(2)
+    for k in range(2):
+        for i in range(19):
+            moved[k, X * i : X * i + 2, :] = pmoved[pl.ds(8 * i + 4 + k, 2, stride=2), :]
 
     loads[4].wait()
     sources, present = [], []
@@ -394,6 +430,8 @@
     halos_r[2].wait_recv()
     halos_r[3].wait_recv()
     cbeyond(cfrom_left, csol_left, PAD - 1)
+    for copy in halos_r + halos_l + sends[0] + sends[1]:
+        copy.wait_send()
     collect(2, outer_l)
     for half in range(2):
         f, span = pasted(
@@ -401,7 +439,7 @@
         for i in range(19):
             settled[i, PAD - 1 : PAD + 1, span] = f[i]
 
-    for copy in halos_r + halos_l + sends[0] + sends[1] + sends[2]:
+    for copy in sends[2]:
         copy.wait_send()
 
 
@@ -450,7 +488,11 @@
                 pltpu.VMEM((C + 2 * PAD, 256), F32),
                 pltpu.VMEM((19, X + 2 * PAD, 256), F32),
                 pltpu.VMEM((19, X + 2 * PAD, 256), F32),
-                pltpu.VMEM((2, 2, 80, 128), F32),
+                pltpu.VMEM((2, 80, 128), F32),
+                pltpu.VMEM((19 * 16, 128), F32),
+                pltpu.VMEM((19 * 16, 128), F32),
+                pltpu.VMEM((16, 128), F32),
+                pltpu.VMEM((160, 128), F32),
                 pltpu.VMEM((256, 128), jnp.bfloat16),
                 pltpu.VMEM((groups, 10, 8, 128), F32),
                 pltpu.VMEM((groups, 24, 128), F32),

time: 27.8 us -> 27.6 us (level)
  no operation moved by 1% of the time
where the time goes in v5:
time: 27.6 us; the launch traced here: 27.4 us
  Pallas kernels  26.8 us (97%)
  between operations  0.64 us (2%)
    pallas_call x1, Pallas kernels, per_device(): pl.pallas_call(body, out_shape=(jax.ShapeDtypeStruct((2, 19 * X, 128), F3...  26 us
    pallas_call x1, Pallas kernels, per_device(): pl.pallas_call(finish, out_shape=(jax.ShapeDtypeStruct(fine_pops.shape, F...  0.81 us

profile of v5, /device:TPU:1, one launch (start us, length us, event | category | flops | bytes accessed | tf_op | source)
XLA Modules:
  0.0 27.4 jit_solution(10180705850987723836)
XLA Ops:
  0.6 26.0 %shard_map.68 = (f32[2,304,128]{2,1,0:T(8,128)S(1)}, f32[19,24,256]{2,1,0:T(8,128)S(1)}) custom-call(s32[8]{0:T(128)} %refs_0_.1, f32[1,19,16,256]{3,2,1,0:T(8,128)} %refs_1_.1, f32[1,16,256]{2,1,0:T(8,128)} %refs_2_.1, f32[1,19,8,256]{3,2,1,0:T(8,128)} %refs_3_.1, f32[1,8,256]{2,1,0:T(8,128)} %refs_4_.1, f32[19,2,2,8,1,128]{5,4,3,2,1,0:T(1,128)} %bitcast.22, ...), custom_call_target="tpu_custom_call" | custom-call | tf_op jit(solution)/shard_map/pallas_call | solution.py:476
  26.6 0.8 %shard_map.69 = (f32[1,19,16,256]{3,2,1,0:T(8,128)}, f32[1,19,8,256]{3,2,1,0:T(8,128)}) custom-call(f32[2,19,16,128]{3,2,1,0:T(8,128)S(1)} %bitcast.21, f32[19,24,256]{2,1,0:T(8,128)S(1)} %get-tuple-element.5.settled), custom_call_target="tpu_custom_call" | custom-call | tf_op jit(solution)/shard_map/pallas_call | solution.py:526

commit v6 on v5

--- a/solution.py
+++ b/solution.py
@@ -144,7 +144,7 @@
 def kernel(
     groups, blocks, slot_hbm, fine_hbm, solid_hbm, coarse_hbm, csolid_hbm,
     fine_view, solid_view, coarse_view, csolid_view, moved, settled,
-    fine, solid, coarse, csolid, first, second, edge, pfirst, psecond, psolid, pmoved, boxes, inner, outer_r, outer_l,
+    fine, solid, coarse, csolid, first, second, edge, pfirst, psecond, psolid, pmoved, means, boxes, inner, outer_r, outer_l,
     from_left, from_right, sol_left, sol_right, cfrom_left, cfrom_right, csol_left, csol_right,
     slot_ref, load_sem, ready, lefts, peers_in, halo_send, halo_recv, box_send, box_recv,
 ):
@@ -233,7 +233,7 @@
     def rescaled(means, rows):
         a = jnp.full((rows, 128), 1.0 - rescale, F32)
         keep = jnp.full((rows, 128), 0.5 * rescale, F32)
-        return relaxed([means[rows * i : rows * i + rows] for i in range(19)], keep, keep, a)
+        return relaxed([means[rows * i : rows * i + rows, :] for i in range(19)], keep, keep, a)
 
     def near(rows):
         return lanes(rows) % 16 < 8
@@ -314,7 +314,8 @@
             first_collision([halo[i, k, :, 0, :] for i in range(19)], s, start, 4, span)
 
     def restricted(sums, outer):
-        f = rescaled(box_means(jnp.concatenate(sums, axis=1)), 2)
+        means[...] = box_means(jnp.concatenate(sums, axis=1))
+        f = rescaled(means, 2)
         for k in range(10):
             outer[g, 2 * k : 2 * k + 2, :] = jnp.where(near(2), f[2 * k], f[min(2 * k + 1, 18)])
 
@@ -418,14 +419,14 @@
     for half in range(2):
         f, span = pasted(half, C, lambda source, k: inner[source, k], PAD)
         for i in range(19):
-            settled[i, PAD : PAD + C, span] = f[i]
+            settled[i, 1 : 1 + C, span] = f[i]
 
     collect(1, outer_r)
     for half in range(2):
         f, span = pasted(
             half, 2, lambda source, k: outer_r[source, 2 * k : 2 * k + 2, :], PAD + C - 1)
         for i in range(19):
-            settled[i, PAD + C - 1 : PAD + C + 1, span] = f[i]
+            settled[i, C : C + 2, span] = f[i]
 
     halos_r[2].wait_recv()
     halos_r[3].wait_recv()
@@ -437,7 +438,7 @@
         f, span = pasted(
             half, 2, lambda source, k: outer_l[source, 2 * k : 2 * k + 2, :], PAD - 1)
         for i in range(19):
-            settled[i, PAD - 1 : PAD + 1, span] = f[i]
+            settled[i, 0:2, span] = f[i]
 
     for copy in sends[2]:
         copy.wait_send()
@@ -450,7 +451,7 @@
     ]
     for store in stores:
         store.start()
-    low, high = streamed(settled, PAD, C)
+    low, high = streamed(settled, 1, C)
     for i in range(19):
         cmoved[i, :, 0:128] = low[i]
         cmoved[i, :, 128:256] = high[i]
@@ -477,7 +478,7 @@
             body,
             out_shape=(
                 jax.ShapeDtypeStruct((2, 19 * X, 128), F32),
-                jax.ShapeDtypeStruct((19, C + 2 * PAD, 256), F32),
+                jax.ShapeDtypeStruct((19, 2 * C, 256), F32),
             ),
             in_specs=[hbm] * 9,
             out_specs=(vmem, vmem),
@@ -493,6 +494,7 @@
                 pltpu.VMEM((19 * 16, 128), F32),
                 pltpu.VMEM((16, 128), F32),
                 pltpu.VMEM((160, 128), F32),
+                pltpu.VMEM((40, 128), F32),
                 pltpu.VMEM((256, 128), jnp.bfloat16),
                 pltpu.VMEM((groups, 10, 8, 128), F32),
                 pltpu.VMEM((groups, 24, 128), F32),

time: 27.6 us -> 27.7 us (level)
  no operation moved by 1% of the time
where the time goes in v6:
time: 27.7 us; the launch traced here: 27.5 us
  Pallas kernels  26.9 us (97%)
  between operations  0.64 us (2%)
    pallas_call x1, Pallas kernels, per_device(): pl.pallas_call(body, out_shape=(jax.ShapeDtypeStruct((2, 19 * X, 128), F3...  26 us
    pallas_call x1, Pallas kernels, per_device(): pl.pallas_call(finish, out_shape=(jax.ShapeDtypeStruct(fine_pops.shape, F...  0.85 us

profile of v6, /device:TPU:1, one launch (start us, length us, event | category | flops | bytes accessed | tf_op | source)
XLA Modules:
  0.0 27.5 jit_solution(874404404456103742)
XLA Ops:
  0.6 26.0 %shard_map.68 = (f32[2,304,128]{2,1,0:T(8,128)S(1)}, f32[19,16,256]{2,1,0:T(8,128)S(1)}) custom-call(s32[8]{0:T(128)} %refs_0_.1, f32[1,19,16,256]{3,2,1,0:T(8,128)} %refs_1_.1, f32[1,16,256]{2,1,0:T(8,128)} %refs_2_.1, f32[1,19,8,256]{3,2,1,0:T(8,128)} %refs_3_.1, f32[1,8,256]{2,1,0:T(8,128)} %refs_4_.1, f32[19,2,2,8,1,128]{5,4,3,2,1,0:T(1,128)} %bitcast.22, ...), custom_call_target="tpu_custom_call" | custom-call | tf_op jit(solution)/shard_map/pallas_call | solution.py:477
  26.6 0.8 %shard_map.69 = (f32[1,19,16,256]{3,2,1,0:T(8,128)}, f32[1,19,8,256]{3,2,1,0:T(8,128)}) custom-call(f32[2,19,16,128]{3,2,1,0:T(8,128)S(1)} %bitcast.21, f32[19,16,256]{2,1,0:T(8,128)S(1)} %get-tuple-element.5.settled), custom_call_target="tpu_custom_call" | custom-call | tf_op jit(solution)/shard_map/pallas_call | solution.py:528

commit v7 on v6

--- a/solution.py
+++ b/solution.py
@@ -241,10 +241,14 @@
     def messages(which, buffer):
         return [
             pltpu.make_async_remote_copy(
-                buffer.at[g], buffer.at[g], box_send.at[which, d], box_recv.at[which, g],
-                peer, MESH)
-            for d, peer in enumerate(peers)
+                buffer.at[g], buffer.at[g], box_send.at[which], box_recv.at[which], peer, MESH)
+            for peer in peers
         ]
+
+    def whole(which, buffer):
+        span = buffer.at[0 : groups - 1]
+        return pltpu.make_async_remote_copy(
+            span, span, box_send.at[which], box_recv.at[which], peers[0], MESH)
 
     sends = [messages(0, inner), messages(1, outer_r), messages(2, outer_l)]
 
@@ -253,10 +257,7 @@
             send.start()
 
     def collect(which, buffer):
-        for d, peer in enumerate(peers):
-            pltpu.make_async_remote_copy(
-                buffer.at[peer[0]], buffer.at[peer[0]], box_send.at[which, d],
-                box_recv.at[which, peer[0]], peer, MESH).wait_recv()
+        whole(which, buffer).wait_recv()
 
     loads[0].wait()
     loads[1].wait()
@@ -431,7 +432,7 @@
     halos_r[2].wait_recv()
     halos_r[3].wait_recv()
     cbeyond(cfrom_left, csol_left, PAD - 1)
-    for copy in halos_r + halos_l + sends[0] + sends[1]:
+    for copy in halos_r + halos_l + [whole(0, inner), whole(1, outer_r)]:
         copy.wait_send()
     collect(2, outer_l)
     for half in range(2):
@@ -440,8 +441,7 @@
         for i in range(19):
             settled[i, 0:2, span] = f[i]
 
-    for copy in sends[2]:
-        copy.wait_send()
+    whole(2, outer_l).wait_send()
 
 
 def finish(moved, settled, fine_out, coarse_out, cmoved, store_sem):
@@ -512,8 +512,8 @@
                 pltpu.SemaphoreType.REGULAR,
                 pltpu.SemaphoreType.DMA((8,)),
                 pltpu.SemaphoreType.DMA((8,)),
-                pltpu.SemaphoreType.DMA((3, groups)),
-                pltpu.SemaphoreType.DMA((3, groups)),
+                pltpu.SemaphoreType.DMA((3,)),
+                pltpu.SemaphoreType.DMA((3,)),
             ],
             compiler_params=pltpu.CompilerParams(
                 collective_id=0, has_side_effects=True, vmem_limit_bytes=16 << 20),

time: 27.7 us -> 27.3 us (0.986)
  Pallas kernels: 26.9 us -> 26.5 us
    pallas_call x1, Pallas kernels: 26 us -> 25.6 us  [per_device(): pl.pallas_call(body, out_shape=(jax.ShapeDtypeStruct((2, 19 * X, 128), F3...]
where the time goes in v7:
time: 27.3 us; the launch traced here: 27.1 us
  Pallas kernels  26.5 us (97%)
  between operations  0.64 us (2%)
    pallas_call x1, Pallas kernels, per_device(): pl.pallas_call(body, out_shape=(jax.ShapeDtypeStruct((2, 19 * X, 128), F3...  25.6 us
    pallas_call x1, Pallas kernels, per_device(): pl.pallas_call(finish, out_shape=(jax.ShapeDtypeStruct(fine_pops.shape, F...  0.85 us

profile of v7, /device:TPU:1, one launch (start us, length us, event | category | flops | bytes accessed | tf_op | source)
XLA Modules:
  0.0 27.1 jit_solution(12266785442951995680)
XLA Ops:
  0.6 25.6 %shard_map.68 = (f32[2,304,128]{2,1,0:T(8,128)S(1)}, f32[19,16,256]{2,1,0:T(8,128)S(1)}) custom-call(s32[8]{0:T(128)} %refs_0_.1, f32[1,19,16,256]{3,2,1,0:T(8,128)} %refs_1_.1, f32[1,16,256]{2,1,0:T(8,128)} %refs_2_.1, f32[1,19,8,256]{3,2,1,0:T(8,128)} %refs_3_.1, f32[1,8,256]{2,1,0:T(8,128)} %refs_4_.1, f32[19,2,2,8,1,128]{5,4,3,2,1,0:T(1,128)} %bitcast.22, ...), custom_call_target="tpu_custom_call" | custom-call | tf_op jit(solution)/shard_map/pallas_call | solution.py:477
  26.3 0.8 %shard_map.69 = (f32[1,19,16,256]{3,2,1,0:T(8,128)}, f32[1,19,8,256]{3,2,1,0:T(8,128)}) custom-call(f32[2,19,16,128]{3,2,1,0:T(8,128)S(1)} %bitcast.21, f32[19,16,256]{2,1,0:T(8,128)S(1)} %get-tuple-element.5.settled), custom_call_target="tpu_custom_call" | custom-call | tf_op jit(solution)/shard_map/pallas_call | solution.py:528
